TPU v7x, 32 devices: a whole 2x2x4 slice. The times are simulated.
32 devices in a mesh: head: 8 (over y, x, core), seq: 4 (over z).
Axes of the slice: x: 2, y: 2, z: 4, core: 2. Of those that a mesh axis runs over, the one named last changes fastest.
Arguments:
- hidden_in: bfloat16 [2, 2048, 2048], P(None, ('head', 'seq')), may hold values from -6 to 6
- doc_lengths: int32 [2, 8], replicated, may hold values from 1 to 1024, 2048 in all within a row
- expert_ids: int32 [2, 2048, 8], P(None, ('head', 'seq')), may hold values from 0 to 15, all different within a row; in each aligned block of 64 rows (0 to 63, 64 to 127, ..., all dimensions but the last counted through in order) at most 48 rows name the same one
- out_grad: bfloat16 [2, 2048, 2048], P(None, ('head', 'seq')), may hold values from -6 to 6
- norm1_gain: bfloat16 [2048], replicated, may hold values from 0.099609375 to 1.8984375
- w_query: bfloat16 [2048, 2048], P(('head', 'seq')), may hold values from -0.125 to 0.125
- w_key: bfloat16 [2048, 2048], P(('head', 'seq')), may hold values from -0.125 to 0.125
- w_value: bfloat16 [2048, 2048], P(('head', 'seq')), may hold values from -0.125 to 0.125
- query_gain: bfloat16 [2048], replicated, may hold values from 0.099609375 to 1.8984375
- key_gain: bfloat16 [2048], replicated, may hold values from 0.099609375 to 1.8984375
- w_out: bfloat16 [2048, 2048], P(('head', 'seq')), may hold values from -2 to 2
- norm2_gain: bfloat16 [2048], replicated, may hold values from 0.099609375 to 1.8984375
- w_router: bfloat16 [2048, 16], replicated, may hold values from -0.0625 to 0.0625
- w_gate: bfloat16 [2048, 16, 1024], P('seq', 'head'), may hold values from -0.125 to 0.125
- w_up: bfloat16 [2048, 16, 1024], P('seq', 'head'), may hold values from -0.125 to 0.125
- w_down: bfloat16 [2048, 16, 1024], P('seq', 'head'), may hold values from -2 to 2
Outputs:
- hidden_out: bfloat16 [2, 2048, 2048], P(None, ('head', 'seq'))
- hidden_grad: bfloat16 [2, 2048, 2048], P(None, ('head', 'seq'))
- grad_norm1_gain: float32 [2048], P(('head', 'seq'))
- grad_w_query: float32 [2048, 2048], P(('head', 'seq'))
- grad_w_key: float32 [2048, 2048], P(('head', 'seq'))
- grad_w_value: float32 [2048, 2048], P(('head', 'seq'))
- grad_query_gain: float32 [2048], P(('head', 'seq'))
- grad_key_gain: float32 [2048], P(('head', 'seq'))
- grad_w_out: float32 [2048, 2048], P(('head', 'seq'))
- grad_norm2_gain: float32 [2048], P(('head', 'seq'))
- grad_w_router: float32 [2048, 16], P(('head', 'seq'))
- grad_w_gate: float32 [2048, 16, 1024], P('seq', 'head')
- grad_w_up: float32 [2048, 16, 1024], P('seq', 'head')
- grad_w_down: float32 [2048, 16, 1024], P('seq', 'head')
Inputs may be any that keep to these rules, and one draw needn't show every extreme that they name: `doc_lengths`: in each micro-batch the 8 document lengths sum to 2048, and the longest is exactly 1024. `expert_ids`: each token names 8 different experts. In each aligned block of 64 tokens of one micro-batch (here half of one device's 128 tokens there) no expert is named more than 48 times, and in some blocks one is named exactly 48 times.
All inputs are finite; a program needn't handle non-finite values.
Results may differ from a plain program's by a relative error of at most 0.025.
Values may be sent and summed in bfloat16 or wider, within the bound.
No kernel may reach another device: no remote copies, remote signals or barrier semaphores. Data moves between devices by JAX's collectives and lax.ppermute only.
A program may use at most 320 MiB of HBM per device.

v0:
```python
import jax
import jax.numpy as jnp
from jax import lax
from jax.sharding import PartitionSpec as P

H = 16
HD = 128
TOPK = 8


eps = 1e-06
rope_base = 10000.0
exact_mode = lax.Precision.HIGHEST


def rms_scale(values):
    return lax.rsqrt(jnp.mean(values * values, axis=-1, keepdims=True) + eps)


def norm_back(grad_normed, normed, scale_rows):
    return scale_rows * (
        grad_normed - normed * jnp.mean(grad_normed * normed, axis=-1, keepdims=True)
    )


def rotate(values, positions, direction):
    half_width = HD // 2
    frequency = rope_base ** (-jnp.arange(half_width, dtype=jnp.float32) * 2.0 / HD)
    angles = positions.astype(jnp.float32)[:, None] * frequency[None, :]
    cosine = jnp.cos(angles)[:, None, :]
    sine_table = direction * jnp.sin(angles)[:, None, :]
    first_half = values[..., :half_width]
    second = values[..., half_width:]
    return jnp.concatenate(
        [first_half * cosine - second * sine_table, second * cosine + first_half * sine_table],
        axis=-1,
    )


def segment_of(positions, lengths):
    starts = jnp.cumsum(lengths) - lengths
    return jnp.sum((positions[:, None] >= starts[None, :]).astype(jnp.int32), axis=1) - 1


def score_block(query_block, seg_block, key_rows, seg_key):
    scores = HD ** (-0.5) * jnp.einsum(
        "qhd,khd->hqk", query_block, key_rows, preferred_element_type=jnp.float32
    )
    return jnp.where((seg_block[:, None] == seg_key[None, :])[None], scores, -1e30)


def attend(queries, key_rows, value_rows, seg_query, seg_key):
    query_count, heads_here, head_width = queries.shape
    block_rows = min(512, query_count)
    block_count = query_count // block_rows

    def one_block(block_args):
        query_block, seg_block = block_args
        scores = score_block(query_block, seg_block, key_rows, seg_key)
        log_total = jax.nn.logsumexp(scores, axis=-1, keepdims=True)
        low_probs = jnp.exp(scores - log_total).astype(jnp.bfloat16)
        mixed_out = jnp.einsum(
            "hqk,khd->qhd", low_probs, value_rows, preferred_element_type=jnp.float32
        )
        return (mixed_out, log_total[..., 0])

    mixed_out, log_totals = lax.map(
        one_block,
        (
            queries.reshape(block_count, block_rows, heads_here, head_width),
            seg_query.reshape(block_count, block_rows),
        ),
    )
    return (mixed_out.reshape(query_count, heads_here * head_width), log_totals)


def attend_back(queries, key_rows, value_rows, seg_query, seg_key, log_totals, grad_mixed):
    query_count, heads_here, head_width = queries.shape
    block_rows = min(512, query_count)
    block_count = query_count // block_rows
    score_scale = HD ** (-0.5)

    def one_block(running, block_args):
        key_sum, value_sum = running
        query_block, seg_block, total_block, grad_block = block_args
        scores = score_block(query_block, seg_block, key_rows, seg_key)
        prob_rows = jnp.exp(scores - total_block[..., None])
        grad_probs = jnp.einsum(
            "qhd,khd->hqk", grad_block, value_rows, preferred_element_type=jnp.float32
        )
        inner_sum = jnp.sum(prob_rows * grad_probs, axis=-1, keepdims=True)
        grad_scores = (prob_rows * (grad_probs - inner_sum)).astype(jnp.bfloat16)
        grad_query = score_scale * jnp.einsum(
            "hqk,khd->qhd", grad_scores, key_rows, preferred_element_type=jnp.float32
        )
        key_sum = key_sum + score_scale * jnp.einsum(
            "hqk,qhd->khd", grad_scores, query_block, preferred_element_type=jnp.float32
        )
        value_sum = value_sum + jnp.einsum(
            "hqk,qhd->khd",
            prob_rows.astype(jnp.bfloat16),
            grad_block,
            preferred_element_type=jnp.float32,
        )
        return ((key_sum, value_sum), grad_query)

    zero_rows = jnp.zeros(key_rows.shape, jnp.float32)
    grad_sums, grad_query = lax.scan(
        one_block,
        (zero_rows, zero_rows),
        (
            queries.reshape(block_count, block_rows, heads_here, head_width),
            seg_query.reshape(block_count, block_rows),
            log_totals,
            grad_mixed.reshape(block_count, block_rows, heads_here, head_width),
        ),
    )
    key_count = key_rows.shape[0]
    return (
        grad_query.reshape(query_count, heads_here * head_width),
        grad_sums[0].reshape(key_count, heads_here * head_width),
        grad_sums[1].reshape(key_count, heads_here * head_width),
    )


def route_tables(routes, router_probs, capacity, experts):
    tokens, chosen = routes.shape
    flat_ids = routes.reshape(tokens * chosen)
    onehot = (flat_ids[:, None] == jnp.arange(experts, dtype=jnp.int32)[None, :]).astype(jnp.int32)
    before = jnp.cumsum(onehot, axis=0) - onehot
    slot_rank = jnp.sum(before * onehot, axis=1)
    slot_index = flat_ids * capacity + slot_rank
    matches = (
        (slot_index[:, None] == jnp.arange(experts * capacity, dtype=jnp.int32)[None, :])
        .astype(jnp.float32)
        .reshape(tokens, chosen, experts * capacity)
    )
    gate_values = jnp.sum(
        onehot.reshape(tokens, chosen, experts).astype(jnp.float32) * router_probs[:, None, :],
        axis=2,
    )
    placed = jnp.sum(matches, axis=1)
    weighted = jnp.sum(matches * gate_values[:, :, None], axis=1)
    return (placed, weighted)


def body(
    hidden_in,
    doc_lengths,
    expert_ids,
    out_grad,
    norm1_gain,
    w_query,
    w_key,
    w_value,
    query_gain,
    key_gain,
    w_out,
    norm2_gain,
    w_router,
    w_gate,
    w_up,
    w_down,
):
    head_count = lax.axis_size("head")
    seq_count = lax.axis_size("seq")
    head_index = lax.axis_index("head")
    seq_index = lax.axis_index("seq")
    micro_count, local_tokens, model_width = hidden_in.shape
    heads_here = H // head_count
    query_rows = local_tokens * head_count
    whole_len = query_rows * seq_count
    experts_here = w_gate.shape[1]
    expert_count = experts_here * head_count
    capacity = max(2, 3 * local_tokens * TOPK // (2 * expert_count))
    slot_count = experts_here * capacity
    stride = seq_count * local_tokens
    local_pos = (
        head_index * stride + seq_index * local_tokens + jnp.arange(local_tokens, dtype=jnp.int32)
    )
    query_range = jnp.arange(query_rows, dtype=jnp.int32)
    query_pos = (
        query_range // local_tokens * stride + seq_index * local_tokens + query_range % local_tokens
    )
    key_range = jnp.arange(whole_len, dtype=jnp.int32)
    key_inner = key_range % query_rows
    key_pos = (
        key_inner // local_tokens * stride
        + key_range // query_rows * local_tokens
        + key_inner % local_tokens
    )
    gain_one = norm1_gain.astype(jnp.float32)
    gain_two = norm2_gain.astype(jnp.float32)
    gain_query = query_gain.astype(jnp.float32)
    gain_key = key_gain.astype(jnp.float32)
    attn_full = (
        lax.all_gather(
            lax.all_gather(w_query, "seq", axis=0, tiled=True), "head", axis=0, tiled=True
        ),
        lax.all_gather(
            lax.all_gather(w_key, "seq", axis=0, tiled=True), "head", axis=0, tiled=True
        ),
        lax.all_gather(
            lax.all_gather(w_value, "seq", axis=0, tiled=True), "head", axis=0, tiled=True
        ),
        lax.all_gather(
            lax.all_gather(w_out, "seq", axis=0, tiled=True), "head", axis=0, tiled=True
        ),
    )
    attn_full, expert_full = (
        attn_full,
        (
            lax.all_gather(w_gate, "seq", axis=0, tiled=True),
            lax.all_gather(w_up, "seq", axis=0, tiled=True),
            lax.all_gather(w_down, "seq", axis=0, tiled=True),
        ),
    )
    saved = []
    out_rows = []
    for micro_index in range(micro_count):
        hidden = hidden_in[micro_index].astype(jnp.float32)
        scale_one = rms_scale(hidden)
        normed_one = hidden * scale_one
        act_one = (normed_one * gain_one).astype(jnp.bfloat16)
        act_proj = act_one
        query_pre = jnp.dot(act_proj, attn_full[0], preferred_element_type=jnp.float32)
        key_pre = jnp.dot(act_proj, attn_full[1], preferred_element_type=jnp.float32)
        value_low = jnp.dot(act_proj, attn_full[2], preferred_element_type=jnp.float32).astype(
            jnp.bfloat16
        )
        query_scale = rms_scale(query_pre)
        key_scale = rms_scale(key_pre)
        query_normed = query_pre * query_scale
        key_normed = key_pre * key_scale
        row_here = query_pre.shape[0]
        query_rot = (
            rotate((query_normed * gain_query).reshape(row_here, -1, HD), local_pos, 1.0)
            .reshape(row_here, -1)
            .astype(jnp.bfloat16)
        )
        key_rot = (
            rotate((key_normed * gain_key).reshape(row_here, -1, HD), local_pos, 1.0)
            .reshape(row_here, -1)
            .astype(jnp.bfloat16)
        )
        query_heads, key_heads, value_heads = (
            lax.all_to_all(query_rot, "head", split_axis=1, concat_axis=0, tiled=True),
            lax.all_to_all(key_rot, "head", split_axis=1, concat_axis=0, tiled=True),
            lax.all_to_all(value_low, "head", split_axis=1, concat_axis=0, tiled=True),
        )
        key_whole, value_whole = (
            lax.all_gather(key_heads, "seq", axis=0, tiled=True),
            lax.all_gather(value_heads, "seq", axis=0, tiled=True),
        )
        seg_query = segment_of(query_pos, doc_lengths[micro_index])
        seg_key = segment_of(key_pos, doc_lengths[micro_index])
        queries = query_heads.reshape(query_rows, heads_here, HD)
        key_rows = key_whole.reshape(whole_len, heads_here, HD)
        value_rows = value_whole.reshape(whole_len, heads_here, HD)
        mixed_out, log_totals = attend(queries, key_rows, value_rows, seg_query, seg_key)
        mixed_low = mixed_out.astype(jnp.bfloat16)
        mixed_tokens = lax.all_to_all(mixed_low, "head", split_axis=0, concat_axis=1, tiled=True)
        branch = jnp.dot(mixed_tokens, attn_full[3], preferred_element_type=jnp.float32)
        residual = hidden + branch
        scale_two = rms_scale(residual)
        normed_two = residual * scale_two
        act_two = (normed_two * gain_two).astype(jnp.bfloat16)
        logits = jnp.dot(act_two, w_router, preferred_element_type=jnp.float32)
        router_probs = jax.nn.softmax(logits, axis=-1)
        placed, weighted = route_tables(
            expert_ids[micro_index], router_probs, capacity, expert_count
        )
        send_rows = jnp.dot(
            placed.T.astype(jnp.bfloat16), act_two, preferred_element_type=jnp.float32
        ).astype(jnp.bfloat16)
        send_grads = jnp.dot(
            weighted.T, out_grad[micro_index].astype(jnp.float32), precision=exact_mode
        ).astype(jnp.bfloat16)
        expert_in, expert_grad_out = (
            lax.all_to_all(
                send_rows.reshape(head_count, slot_count, model_width),
                "head",
                split_axis=0,
                concat_axis=0,
                tiled=True,
            ),
            lax.all_to_all(
                send_grads.reshape(head_count, slot_count, model_width),
                "head",
                split_axis=0,
                concat_axis=0,
                tiled=True,
            ),
        )
        expert_in = expert_in.reshape(head_count, experts_here, capacity, model_width)
        expert_grad_out = expert_grad_out.reshape(head_count, experts_here, capacity, model_width)
        gate_pre = jnp.einsum(
            "secd,def->secf", expert_in, expert_full[0], preferred_element_type=jnp.float32
        )
        upward = jnp.einsum(
            "secd,def->secf", expert_in, expert_full[1], preferred_element_type=jnp.float32
        )
        inner_act = (jax.nn.silu(gate_pre) * upward).astype(jnp.bfloat16)
        expert_out = jnp.einsum(
            "secf,def->secd", inner_act, expert_full[2], preferred_element_type=jnp.float32
        ).astype(jnp.bfloat16)
        returned = lax.all_to_all(
            expert_out.reshape(head_count, slot_count, model_width),
            "head",
            split_axis=0,
            concat_axis=0,
            tiled=True,
        )
        returned = returned.reshape(expert_count * capacity, model_width)
        expert_sum = jnp.dot(weighted, returned.astype(jnp.float32), precision=exact_mode)
        out_rows.append((residual + expert_sum).astype(jnp.bfloat16))
        saved.append(
            (
                scale_one,
                normed_one,
                act_proj,
                query_scale,
                key_scale,
                query_normed,
                key_normed,
                queries,
                key_rows,
                value_rows,
                seg_query,
                seg_key,
                log_totals,
                mixed_tokens,
                scale_two,
                normed_two,
                act_two,
                router_probs,
                placed,
                returned,
                expert_in,
                expert_grad_out,
                gate_pre,
                upward,
                inner_act,
            )
        )
    grad_rows = []
    grad_totals = None
    for micro_index in range(micro_count):
        (
            scale_one,
            normed_one,
            act_proj,
            query_scale,
            key_scale,
            query_normed,
            key_normed,
            queries,
            key_rows,
            value_rows,
            seg_query,
            seg_key,
            log_totals,
            mixed_tokens,
            scale_two,
            normed_two,
            act_two,
            router_probs,
            placed,
            returned,
            expert_in,
            expert_grad_out,
            gate_pre,
            upward,
            inner_act,
        ) = saved[micro_index]
        grad_low = out_grad[micro_index]
        grad_inner = jnp.einsum(
            "secd,def->secf", expert_grad_out, expert_full[2], preferred_element_type=jnp.float32
        )
        grad_w_down = jnp.einsum(
            "secd,secf->def", expert_grad_out, inner_act, preferred_element_type=jnp.float32
        )
        sigmoid_gate = jax.nn.sigmoid(gate_pre)
        grad_gate_pre = (
            grad_inner * upward * sigmoid_gate * (1.0 + gate_pre * (1.0 - sigmoid_gate))
        ).astype(jnp.bfloat16)
        grad_upward = (grad_inner * gate_pre * sigmoid_gate).astype(jnp.bfloat16)
        grad_w_gate = jnp.einsum(
            "secd,secf->def", expert_in, grad_gate_pre, preferred_element_type=jnp.float32
        )
        grad_w_up = jnp.einsum(
            "secd,secf->def", expert_in, grad_upward, preferred_element_type=jnp.float32
        )
        grad_copy = jnp.einsum(
            "secf,def->secd", grad_gate_pre, expert_full[0], preferred_element_type=jnp.float32
        ) + jnp.einsum(
            "secf,def->secd", grad_upward, expert_full[1], preferred_element_type=jnp.float32
        )
        grad_back = lax.all_to_all(
            grad_copy.astype(jnp.bfloat16).reshape(head_count, slot_count, model_width),
            "head",
            split_axis=0,
            concat_axis=0,
            tiled=True,
        )
        grad_back = grad_back.reshape(expert_count * capacity, model_width)
        grad_act_two = jnp.dot(
            placed.astype(jnp.bfloat16), grad_back, preferred_element_type=jnp.float32
        )
        slot_scores = jnp.einsum(
            "td,sd->ts", grad_low, returned, preferred_element_type=jnp.float32
        )
        grad_router = jnp.sum(
            (slot_scores * placed).reshape(local_tokens, expert_count, capacity), axis=2
        )
        grad_logits = (
            router_probs
            * (grad_router - jnp.sum(router_probs * grad_router, axis=-1, keepdims=True))
        ).astype(jnp.bfloat16)
        grad_w_router = jnp.einsum(
            "td,te->de", act_two, grad_logits, preferred_element_type=jnp.float32
        )
        grad_act_two = grad_act_two + jnp.einsum(
            "te,de->td", grad_logits, w_router, preferred_element_type=jnp.float32
        )
        grad_gain_two = jnp.sum(grad_act_two * normed_two, axis=0)
        grad_residual = grad_low.astype(jnp.float32) + norm_back(
            grad_act_two * gain_two, normed_two, scale_two
        )
        grad_branch = grad_residual.astype(jnp.bfloat16)
        grad_w_out = jnp.einsum(
            "tc,td->cd", mixed_tokens, grad_branch, preferred_element_type=jnp.float32
        )
        grad_mixed = jnp.einsum(
            "td,cd->tc", grad_branch, attn_full[3], preferred_element_type=jnp.float32
        ).astype(jnp.bfloat16)
        grad_heads = lax.all_to_all(grad_mixed, "head", split_axis=1, concat_axis=0, tiled=True)
        grad_query, grad_key_all, grad_value_all = attend_back(
            queries,
            key_rows,
            value_rows,
            seg_query,
            seg_key,
            log_totals,
            grad_heads.reshape(query_rows, heads_here, HD),
        )
        key_part, value_part = (
            lax.psum_scatter(
                grad_key_all.astype(jnp.bfloat16), "seq", scatter_dimension=0, tiled=True
            ).astype(jnp.float32),
            lax.psum_scatter(
                grad_value_all.astype(jnp.bfloat16), "seq", scatter_dimension=0, tiled=True
            ).astype(jnp.float32),
        )
        back_query, back_key, back_value = (
            lax.all_to_all(
                grad_query.astype(jnp.bfloat16), "head", split_axis=0, concat_axis=1, tiled=True
            ),
            lax.all_to_all(
                key_part.astype(jnp.bfloat16), "head", split_axis=0, concat_axis=1, tiled=True
            ),
            lax.all_to_all(
                value_part.astype(jnp.bfloat16), "head", split_axis=0, concat_axis=1, tiled=True
            ),
        )
        row_here = back_query.shape[0]
        grad_query_rot = rotate(
            back_query.astype(jnp.float32).reshape(row_here, -1, HD), local_pos, -1.0
        ).reshape(row_here, -1)
        grad_key_rot = rotate(
            back_key.astype(jnp.float32).reshape(row_here, -1, HD), local_pos, -1.0
        ).reshape(row_here, -1)
        grad_gain_query = jnp.sum(grad_query_rot * query_normed, axis=0)
        grad_gain_key = jnp.sum(grad_key_rot * key_normed, axis=0)
        pull_query = grad_query_rot * gain_query
        pull_key = grad_key_rot * gain_key
        inner_query = jnp.mean(pull_query * query_normed, axis=-1, keepdims=True)
        inner_key = jnp.mean(pull_key * key_normed, axis=-1, keepdims=True)
        grad_query_pre = (query_scale * (pull_query - query_normed * inner_query)).astype(
            jnp.bfloat16
        )
        grad_key_pre = (key_scale * (pull_key - key_normed * inner_key)).astype(jnp.bfloat16)
        grad_w_query = jnp.einsum(
            "td,tc->dc", act_proj, grad_query_pre, preferred_element_type=jnp.float32
        )
        grad_w_key = jnp.einsum(
            "td,tc->dc", act_proj, grad_key_pre, preferred_element_type=jnp.float32
        )
        grad_w_value = jnp.einsum(
            "td,tc->dc", act_proj, back_value, preferred_element_type=jnp.float32
        )
        grad_act_one = jnp.einsum(
            "tc,dc->td", grad_query_pre, attn_full[0], preferred_element_type=jnp.float32
        )
        grad_act_one = grad_act_one + jnp.einsum(
            "tc,dc->td", grad_key_pre, attn_full[1], preferred_element_type=jnp.float32
        )
        grad_act_one = grad_act_one + jnp.einsum(
            "tc,dc->td", back_value, attn_full[2], preferred_element_type=jnp.float32
        )
        grad_gain_one = jnp.sum(grad_act_one * normed_one, axis=0)
        grad_hidden = grad_residual + norm_back(grad_act_one * gain_one, normed_one, scale_one)
        grad_rows.append(grad_hidden.astype(jnp.bfloat16))
        grad_parts = (
            grad_gain_one,
            grad_w_query,
            grad_w_key,
            grad_w_value,
            grad_gain_query,
            grad_gain_key,
            grad_w_out,
            grad_gain_two,
            grad_w_router,
            grad_w_gate,
            grad_w_up,
            grad_w_down,
        )
        grad_totals = (
            grad_parts
            if grad_totals is None
            else tuple((earlier + later for earlier, later in zip(grad_totals, grad_parts)))
        )
    grad_totals = (
        lax.psum_scatter(
            lax.psum_scatter(
                grad_totals[0].astype(jnp.bfloat16), "head", scatter_dimension=0, tiled=True
            ),
            "seq",
            scatter_dimension=0,
            tiled=True,
        ).astype(jnp.float32),
        lax.psum_scatter(
            lax.psum_scatter(
                grad_totals[1].astype(jnp.bfloat16), "head", scatter_dimension=0, tiled=True
            ),
            "seq",
            scatter_dimension=0,
            tiled=True,
        ).astype(jnp.float32),
        lax.psum_scatter(
            lax.psum_scatter(
                grad_totals[2].astype(jnp.bfloat16), "head", scatter_dimension=0, tiled=True
            ),
            "seq",
            scatter_dimension=0,
            tiled=True,
        ).astype(jnp.float32),
        lax.psum_scatter(
            lax.psum_scatter(
                grad_totals[3].astype(jnp.bfloat16), "head", scatter_dimension=0, tiled=True
            ),
            "seq",
            scatter_dimension=0,
            tiled=True,
        ).astype(jnp.float32),
        lax.psum_scatter(
            lax.psum_scatter(
                grad_totals[4].astype(jnp.bfloat16), "head", scatter_dimension=0, tiled=True
            ),
            "seq",
            scatter_dimension=0,
            tiled=True,
        ).astype(jnp.float32),
        lax.psum_scatter(
            lax.psum_scatter(
                grad_totals[5].astype(jnp.bfloat16), "head", scatter_dimension=0, tiled=True
            ),
            "seq",
            scatter_dimension=0,
            tiled=True,
        ).astype(jnp.float32),
        lax.psum_scatter(
            lax.psum_scatter(
                grad_totals[6].astype(jnp.bfloat16), "head", scatter_dimension=0, tiled=True
            ),
            "seq",
            scatter_dimension=0,
            tiled=True,
        ).astype(jnp.float32),
        lax.psum_scatter(
            lax.psum_scatter(
                grad_totals[7].astype(jnp.bfloat16), "head", scatter_dimension=0, tiled=True
            ),
            "seq",
            scatter_dimension=0,
            tiled=True,
        ).astype(jnp.float32),
        lax.psum_scatter(
            lax.psum_scatter(
                grad_totals[8].astype(jnp.bfloat16), "head", scatter_dimension=0, tiled=True
            ),
            "seq",
            scatter_dimension=0,
            tiled=True,
        ).astype(jnp.float32),
        lax.psum_scatter(
            grad_totals[9].astype(jnp.bfloat16), "seq", scatter_dimension=0, tiled=True
        ).astype(jnp.float32),
        lax.psum_scatter(
            grad_totals[10].astype(jnp.bfloat16), "seq", scatter_dimension=0, tiled=True
        ).astype(jnp.float32),
        lax.psum_scatter(
            grad_totals[11].astype(jnp.bfloat16), "seq", scatter_dimension=0, tiled=True
        ).astype(jnp.float32),
    )
    return (
        jnp.stack(out_rows),
        jnp.stack(grad_rows),
        grad_totals[0],
        grad_totals[1],
        grad_totals[2],
        grad_totals[3],
        grad_totals[4],
        grad_totals[5],
        grad_totals[6],
        grad_totals[7],
        grad_totals[8],
        grad_totals[9],
        grad_totals[10],
        grad_totals[11],
    )


def solution(mesh):
    in_specs = (
        P(None, ("head", "seq"), None),
        P(),
        P(None, ("head", "seq"), None),
        P(None, ("head", "seq"), None),
        P(),
        P(("head", "seq"), None),
        P(("head", "seq"), None),
        P(("head", "seq"), None),
        P(),
        P(),
        P(("head", "seq"), None),
        P(),
        P(),
        P("seq", "head", None),
        P("seq", "head", None),
        P("seq", "head", None),
    )
    out_specs = (
        P(None, ("head", "seq"), None),
        P(None, ("head", "seq"), None),
        P(("head", "seq")),
        P(("head", "seq"), None),
        P(("head", "seq"), None),
        P(("head", "seq"), None),
        P(("head", "seq")),
        P(("head", "seq")),
        P(("head", "seq"), None),
        P(("head", "seq")),
        P(("head", "seq"), None),
        P("seq", "head", None),
        P("seq", "head", None),
        P("seq", "head", None),
    )
    return jax.shard_map(body, mesh=mesh, in_specs=in_specs, out_specs=out_specs, check_vma=False)
```

profile of v0, /device:TPU:0, one launch (start us, length us, event | category | flops | bytes accessed | tf_op | source)
XLA Modules:
  0.0 2288.2 jit_solution(2433724499459935469)
XLA Ops:
  9.5 30.8 %all-gather.16.cloned.1.call-done = bf16[256,2048]{1,0:T(8,128)(2,1)} async-done(((bf16[64,2048]{1,0:T(8,128)(2,1)}), bf16[256,2048]{1,0:T(8,128)(2,1)}) %all-gather.16.cloned.1.call-update) | async-done | bytes 1048592 | tf_op jit(solution)/shard_map/all_gather | solution.py:204
  40.3 29.0 %all-gather.26.cloned.1.call-done = bf16[256,2048]{1,0:T(8,128)(2,1)} async-done(((bf16[64,2048]{1,0:T(8,128)(2,1)}), bf16[256,2048]{1,0:T(8,128)(2,1)}) %all-gather.26.cloned.1.call-update) | async-done | bytes 1048592 | tf_op jit(solution)/shard_map/all_gather | solution.py:201
  69.4 29.0 %all-gather.22.cloned.1.call-done = bf16[256,2048]{1,0:T(8,128)(2,1)} async-done(((bf16[64,2048]{1,0:T(8,128)(2,1)}), bf16[256,2048]{1,0:T(8,128)(2,1)}) %all-gather.22.cloned.1.call-update) | async-done | bytes 1048592 | tf_op jit(solution)/shard_map/all_gather | solution.py:198
  103.3 50.7 %all-gather.18.cloned.1.call-done = bf16[2048,2048]{1,0:T(8,128)(2,1)} async-done(((bf16[256,2048]{1,0:T(8,128)(2,1)}), bf16[2048,2048]{1,0:T(8,128)(2,1)}) %all-gather.18.cloned.1.call-update) | async-done | bytes 8388624 | tf_op jit(solution)/shard_map/all_gather | solution.py:203
  163.3 49.3 %all-gather.28.cloned.1.call-done = bf16[2048,2048]{1,0:T(8,128)(2,1)} async-done(((bf16[256,2048]{1,0:T(8,128)(2,1)}), bf16[2048,2048]{1,0:T(8,128)(2,1)}) %all-gather.28.cloned.1.call-update) | async-done | bytes 8388624 | tf_op jit(solution)/shard_map/all_gather | solution.py:200
  220.2 48.7 %all-gather.24.cloned.1.call-done = bf16[2048,2048]{1,0:T(8,128)(2,1)} async-done(((bf16[256,2048]{1,0:T(8,128)(2,1)}), bf16[2048,2048]{1,0:T(8,128)(2,1)}) %all-gather.24.cloned.1.call-update) | async-done | bytes 8388624 | tf_op jit(solution)/shard_map/all_gather | solution.py:197
  386.8 30.4 %all-gather.34.cloned.1.call-done = bf16[2048,2048]{1,0:T(8,128)(2,1)} async-done(((bf16[256,2048]{1,0:T(8,128)(2,1)}), bf16[2048,2048]{1,0:T(8,128)(2,1)}) %all-gather.34.cloned.1.call-update) | async-done | bytes 8388624 | tf_op jit(solution)/shard_map/all_gather | solution.py:206
  432.0 13.4 all-gather.44.cloned.1.call-done
  483.8 141.8 %all-gather.38.cloned.1.call-done = bf16[2048,2,1024]{2,0,1:T(8,128)(2,1)} async-done(((bf16[512,2,1024]{2,0,1:T(8,128)(2,1)}), bf16[2048,2,1024]{2,0,1:T(8,128)(2,1)}) %all-gather.38.cloned.1.call-update) | async-done | bytes 8388624 | tf_op jit(solution)/shard_map/all_gather | solution.py:214
  635.0 139.9 %all-gather.36.cloned.1.call-done = bf16[2048,2,1024]{2,0,1:T(8,128)(2,1)} async-done(((bf16[512,2,1024]{2,0,1:T(8,128)(2,1)}), bf16[2048,2,1024]{2,0,1:T(8,128)(2,1)}) %all-gather.36.cloned.1.call-update) | async-done | bytes 8388624 | tf_op jit(solution)/shard_map/all_gather | solution.py:213
  788.2 135.9 %all-gather.40.cloned.1.call-done = bf16[2048,2,1024]{2,0,1:T(8,128)(2,1)} async-done(((bf16[512,2,1024]{2,0,1:T(8,128)(2,1)}), bf16[2048,2,1024]{2,0,1:T(8,128)(2,1)}) %all-gather.40.cloned.1.call-update) | async-done | bytes 8388624 | tf_op jit(solution)/shard_map/all_gather | solution.py:215
  962.2 22.1 all-to-all-done.5
  1004.7 22.5 all-to-all-done.13
  1047.0 32.9 %all-to-all-done.10 = bf16[8,96,2048]{2,1,0:T(8,128)(2,1)} async-done(((bf16[8,96,2048]{2,1,0:T(8,128)(2,1)}), bf16[8,96,2048]{2,1,0:T(8,128)(2,1)}, u32[]{:S(2)}, u32[]{:S(2)}) %all-to-all-start.10) | async-done | bytes 3145760 | tf_op jit(solution)/shard_map/all_to_all | solution.py:280
  1103.4 19.1 all-to-all-done.18
  1166.8 22.1 all-to-all-done.11
  1198.9 32.4 %all-to-all-done.19 = bf16[8,96,2048]{2,1,0:T(8,128)(2,1)} async-done(((bf16[8,96,2048]{2,1,0:T(8,128)(2,1)}), bf16[8,96,2048]{2,1,0:T(8,128)(2,1)}, u32[]{:S(2)}, u32[]{:S(2)}) %all-to-all-start.19) | async-done | bytes 3145760 | tf_op jit(solution)/shard_map/all_to_all | solution.py:399
  1482.2 15.7 fusion.78
  1498.0 15.3 fusion.5
  1526.6 15.3 fusion.3
  1555.0 15.1 fusion.4
  1597.6 50.3 %reduce-scatter.32.cloned.1.call-done = bf16[256,2048]{1,0:T(8,128)(2,1)} async-done(((bf16[2048,2048]{1,0:T(8,128)(2,1)}), bf16[256,2048]{1,0:T(8,128)(2,1)}) %reduce-scatter.32.cloned.1.call-update) | async-done | bytes 1048592 | tf_op jit(solution)/shard_map/reduce_scatter | solution.py:541
  1666.8 56.2 %reduce-scatter.28.cloned.1.call-done = bf16[256,2048]{1,0:T(8,128)(2,1)} async-done(((bf16[2048,2048]{1,0:T(8,128)(2,1)}), bf16[256,2048]{1,0:T(8,128)(2,1)}) %reduce-scatter.28.cloned.1.call-update) | async-done | bytes 1048592 | tf_op jit(solution)/shard_map/reduce_scatter | solution.py:533
  1723.1 23.9 %all-reduce.8 = (bf16[2048]{0:T(1024)(128)(2,1)S(1)}, bf16[2048]{0:T(1024)(128)(2,1)S(1)}, bf16[2048]{0:T(1024)(128)(2,1)S(1)}, bf16[2048]{0:T(1024)(128)(2,1)S(1)}) all-reduce(bf16[2048]{0:T(1024)(128)(2,1)S(1)} %add_convert_fusion.13, ...), channel_id=6, replica_groups=mesh['head'=8,'seq'=4] {'head'}, use_global_device_ids=true, to_apply=%region_54.55.clone | all-reduce | flops 8192 | bytes 32768
  1747.3 13.0 all-reduce.9
  1763.8 106.2 %reduce-scatter.50.cloned.1.call-done = bf16[512,2,1024]{0,2,1:T(8,128)(2,1)} async-done(((bf16[2048,2,1024]{0,2,1:T(8,128)(2,1)}), bf16[512,2,1024]{0,2,1:T(8,128)(2,1)}) %reduce-scatter.50.cloned.1.call-update) | async-done | bytes 2097168 | tf_op jit(solution)/shard_map/reduce_scatter | solution.py:602
  1876.5 141.0 %reduce-scatter.46.cloned.1.call-done = bf16[512,2,1024]{0,2,1:T(8,128)(2,1)} async-done(((bf16[2048,2,1024]{0,2,1:T(8,128)(2,1)}), bf16[512,2,1024]{0,2,1:T(8,128)(2,1)}) %reduce-scatter.46.cloned.1.call-update) | async-done | bytes 2097168 | tf_op jit(solution)/shard_map/reduce_scatter | solution.py:596
  2024.0 141.1 %reduce-scatter.48.cloned.1.call-done = bf16[512,2,1024]{0,2,1:T(8,128)(2,1)} async-done(((bf16[2048,2,1024]{0,2,1:T(8,128)(2,1)}), bf16[512,2,1024]{0,2,1:T(8,128)(2,1)}) %reduce-scatter.48.cloned.1.call-update) | async-done | bytes 2097168 | tf_op jit(solution)/shard_map/reduce_scatter | solution.py:599
  2171.5 23.7 %reduce-scatter.42.cloned.1.call-done = bf16[64,2048]{1,0:T(8,128)(2,1)} async-done(((bf16[256,2048]{1,0:T(8,128)(2,1)}), bf16[64,2048]{1,0:T(8,128)(2,1)}) %reduce-scatter.42.cloned.1.call-update) | async-done | bytes 262160 | tf_op jit(solution)/shard_map/reduce_scatter | solution.py:572
  2197.0 26.3 %reduce-scatter.38.cloned.1.call-done = bf16[64,2048]{1,0:T(8,128)(2,1)} async-done(((bf16[256,2048]{1,0:T(8,128)(2,1)}), bf16[64,2048]{1,0:T(8,128)(2,1)}) %reduce-scatter.38.cloned.1.call-update) | async-done | bytes 262160 | tf_op jit(solution)/shard_map/reduce_scatter | solution.py:548
  2225.1 26.4 %reduce-scatter.34.cloned.1.call-done = bf16[64,2048]{1,0:T(8,128)(2,1)} async-done(((bf16[256,2048]{1,0:T(8,128)(2,1)}), bf16[64,2048]{1,0:T(8,128)(2,1)}) %reduce-scatter.34.cloned.1.call-update) | async-done | bytes 262160 | tf_op jit(solution)/shard_map/reduce_scatter | solution.py:540
  2253.2 26.4 %reduce-scatter.30.cloned.1.call-done = bf16[64,2048]{1,0:T(8,128)(2,1)} async-done(((bf16[256,2048]{1,0:T(8,128)(2,1)}), bf16[64,2048]{1,0:T(8,128)(2,1)}) %reduce-scatter.30.cloned.1.call-update) | async-done | bytes 262160 | tf_op jit(solution)/shard_map/reduce_scatter | solution.py:532
  (564 shorter events, 724.7 us)
Async XLA Ops:
  8.7 89.6 %all-gather.22.cloned.1.call-start = ((), (), s32[]{:S(2)}) async-start(), calls=%async_computation.44 | async-start | bytes 1310720 | tf_op jit(solution)/shard_map/all_gather | solution.py:198
  9.4 144.6 %all-gather.18.cloned.1.call-start = ((), (), s32[]{:S(2)}) async-start(), calls=%async_computation.42 | async-start | bytes 9437184 | tf_op jit(solution)/shard_map/all_gather | solution.py:203
  40.3 172.3 %all-gather.28.cloned.1.call-start = ((), (), s32[]{:S(2)}) async-start(), calls=%async_computation.47 | async-start | bytes 9437184 | tf_op jit(solution)/shard_map/all_gather | solution.py:200
  69.3 199.5 %all-gather.24.cloned.1.call-start = ((), (), s32[]{:S(2)}) async-start(), calls=%async_computation.45 | async-start | bytes 9437184 | tf_op jit(solution)/shard_map/all_gather | solution.py:197
  98.3 200.0 %all-gather.32.cloned.1.call-start = ((), (), s32[]{:S(2)}) async-start(), calls=%async_computation.49 | async-start | bytes 1310720 | tf_op jit(solution)/shard_map/all_gather | solution.py:207
  159.9 114.5 %all-to-all-start = ((bf16[64,8,256]{2,0,1:T(8,128)(2,1)}), bf16[64,8,256]{2,0,1:T(8,128)(2,1)S(1)}, u32[]{:S(2)}, u32[]{:S(2)}) async-start(bf16[64,8,256]{2,0,1:T(8,128)(2,1)} %bitcast.597), calls=%async_computation | async-start | bytes 524288 | tf_op jit(solution)/shard_map/all_to_all | solution.py:249
  163.3 186.3 %all-gather.20.cloned.1.call-start = ((), (), s32[]{:S(2)}) async-start(), calls=%async_computation.43 | async-start | bytes 1310720 | tf_op jit(solution)/shard_map/all_gather | solution.py:253
  293.4 123.8 %all-gather.34.cloned.1.call-start = ((), (), s32[]{:S(2)}) async-start(), calls=%async_computation.50 | async-start | bytes 9437184 | tf_op jit(solution)/shard_map/all_gather | solution.py:206
  298.4 147.0 %all-gather.44.cloned.1.call-start = ((), (), s32[]{:S(2)}) async-start(), calls=%async_computation.55 | async-start | bytes 1310720 | tf_op jit(solution)/shard_map/all_gather | solution.py:252
  310.2 164.0 %all-gather.42.cloned.1.call-start = ((), (), s32[]{:S(2)}) async-start(), calls=%async_computation.54 | async-start | bytes 1310720 | tf_op jit(solution)/shard_map/all_gather | solution.py:253
  325.5 300.0 %all-gather.38.cloned.1.call-start = ((), (), s32[]{:S(2)}) async-start(), calls=%async_computation.52 | async-start | bytes 10485760 | tf_op jit(solution)/shard_map/all_gather | solution.py:214
  329.2 445.7 %all-gather.36.cloned.1.call-start = ((), (), s32[]{:S(2)}) async-start(), calls=%async_computation.51 | async-start | bytes 10485760 | tf_op jit(solution)/shard_map/all_gather | solution.py:213
  331.6 592.5 %all-gather.40.cloned.1.call-start = ((), (), s32[]{:S(2)}) async-start(), calls=%async_computation.53 | async-start | bytes 10485760 | tf_op jit(solution)/shard_map/all_gather | solution.py:215
  468.9 315.3 %all-to-all-start.12 = ((bf16[8,96,2048]{2,1,0:T(8,128)(2,1)}), bf16[8,96,2048]{2,1,0:T(8,128)(2,1)}, u32[]{:S(2)}, u32[]{:S(2)}) async-start(bf16[8,96,2048]{2,1,0:T(8,128)(2,1)} %bitcast.602), calls=%async_computation.12 | async-start | bytes 6291456 | tf_op jit(solution)/shard_map/all_to_all | solution.py:287
  784.3 157.7 %all-to-all-start.9 = ((bf16[8,64,256]{2,1,0:T(8,128)(2,1)}), bf16[8,64,256]{2,1,0:T(8,128)(2,1)S(1)}, u32[]{:S(2)}, u32[]{:S(2)}) async-start(bf16[8,64,256]{2,1,0:T(8,128)(2,1)} %convert_element_type.519), calls=%async_computation.9 | async-start | bytes 524288 | tf_op jit(solution)/shard_map/all_to_all | solution.py:262
  1193.4 151.2 %reduce-scatter.26.cloned.1.call-start = ((), (), s32[]{:S(2)}) async-start(), calls=%async_computation.59 | async-start | bytes 1310720 | tf_op jit(solution)/shard_map/reduce_scatter | solution.py:451
  1262.2 85.8 %reduce-scatter.22.cloned.1.call-start = ((), (), s32[]{:S(2)}) async-start(), calls=%async_computation.57 | async-start | bytes 1310720 | tf_op jit(solution)/shard_map/reduce_scatter | solution.py:451
  1290.0 95.1 %reduce-scatter.44.cloned.1.call-start = ((), (), s32[]{:S(2)}) async-start(), calls=%async_computation.68 | async-start | bytes 73728 | tf_op jit(solution)/shard_map/reduce_scatter | solution.py:589
  1292.0 120.5 %reduce-scatter.20.cloned.1.call-start = ((), (), s32[]{:S(2)}) async-start(), calls=%async_computation.56 | async-start | bytes 1310720 | tf_op jit(solution)/shard_map/reduce_scatter | solution.py:448
  1310.1 106.2 %reduce-scatter.24.cloned.1.call-start = ((), (), s32[]{:S(2)}) async-start(), calls=%async_computation.58 | async-start | bytes 1310720 | tf_op jit(solution)/shard_map/reduce_scatter | solution.py:448
  1324.7 245.6 %reduce-scatter.40.cloned.1.call-start = ((), (), s32[]{:S(2)}) async-start(), calls=%async_computation.66 | async-start | bytes 9437184 | tf_op jit(solution)/shard_map/reduce_scatter | solution.py:573
  1358.3 215.2 %reduce-scatter.36.cloned.1.call-start = ((), (), s32[]{:S(2)}) async-start(), calls=%async_computation.64 | async-start | bytes 9437184 | tf_op jit(solution)/shard_map/reduce_scatter | solution.py:549
  1385.1 196.9 %reduce-scatter.52.cloned.1.call-start = ((), (), s32[]{:S(2)}) async-start(), calls=%async_computation.72 | async-start | bytes 81920
  1426.2 221.7 %reduce-scatter.32.cloned.1.call-start = ((), (), s32[]{:S(2)}) async-start(), calls=%async_computation.62 | async-start | bytes 9437184 | tf_op jit(solution)/shard_map/reduce_scatter | solution.py:541
  1459.1 263.9 %reduce-scatter.28.cloned.1.call-start = ((), (), s32[]{:S(2)}) async-start(), calls=%async_computation.60 | async-start | bytes 9437184 | tf_op jit(solution)/shard_map/reduce_scatter | solution.py:533
  1482.0 388.1 %reduce-scatter.50.cloned.1.call-start = ((), (), s32[]{:S(2)}) async-start(), calls=%async_computation.71 | async-start | bytes 10485760 | tf_op jit(solution)/shard_map/reduce_scatter | solution.py:602
  1513.3 504.2 %reduce-scatter.46.cloned.1.call-start = ((), (), s32[]{:S(2)}) async-start(), calls=%async_computation.69 | async-start | bytes 10485760 | tf_op jit(solution)/shard_map/reduce_scatter | solution.py:596
  1541.9 623.2 %reduce-scatter.48.cloned.1.call-start = ((), (), s32[]{:S(2)}) async-start(), calls=%async_computation.70 | async-start | bytes 10485760 | tf_op jit(solution)/shard_map/reduce_scatter | solution.py:599
  1570.2 625.1 %reduce-scatter.42.cloned.1.call-start = ((), (), s32[]{:S(2)}) async-start(), calls=%async_computation.67 | async-start | bytes 1310720 | tf_op jit(solution)/shard_map/reduce_scatter | solution.py:572
  1570.9 652.4 %reduce-scatter.38.cloned.1.call-start = ((), (), s32[]{:S(2)}) async-start(), calls=%async_computation.65 | async-start | bytes 1310720 | tf_op jit(solution)/shard_map/reduce_scatter | solution.py:548
  1573.5 677.9 %reduce-scatter.34.cloned.1.call-start = ((), (), s32[]{:S(2)}) async-start(), calls=%async_computation.63 | async-start | bytes 1310720 | tf_op jit(solution)/shard_map/reduce_scatter | solution.py:540
  1647.9 631.8 %reduce-scatter.30.cloned.1.call-start = ((), (), s32[]{:S(2)}) async-start(), calls=%async_computation.61 | async-start | bytes 1310720 | tf_op jit(solution)/shard_map/reduce_scatter | solution.py:532
  (112 other events, 4652.4 us)
Sparse Core Ops, SparseCore 0:
  9.6 30.6 all-gather.15
  41.8 27.4 all-gather.25
  70.9 27.4 all-gather.21
  100.1 53.8 all-gather.17
  155.7 56.8 all-gather.27
  214.4 54.4 all-gather.23
  270.4 27.9 all-gather.31
  300.5 27.4 all-gather.19
  329.5 27.3 all-gather.29
  358.6 58.5 all-gather.33
  418.8 26.5 all-gather.43
  446.8 27.4 all-gather.41
  476.4 149.1 all-gather.37
  627.0 147.8 all-gather.35
  776.3 147.8 all-gather.39
  1262.4 23.5 reduce-scatter.25
  1290.2 23.8 reduce-scatter.21
  1317.5 30.0 reduce-scatter.43
  1350.0 27.1 reduce-scatter.19
  1379.3 25.7 reduce-scatter.23
  1409.0 69.9 reduce-scatter.39
  1482.4 71.2 reduce-scatter.35
  1556.0 18.9 reduce-scatter.51
  1578.3 69.5 reduce-scatter.31
  1651.7 71.2 reduce-scatter.27
  1725.2 144.7 reduce-scatter.49
  1872.2 145.1 reduce-scatter.45
  2019.8 145.1 reduce-scatter.47
  2167.4 27.8 reduce-scatter.41
  2197.5 25.7 reduce-scatter.37
  2225.6 25.7 reduce-scatter.33
  2253.9 25.7 reduce-scatter.29
where the time goes:
time: 2300 us; the launch traced here: 2290 us
  waiting for transfers between devices  1520 us (66%)
  matrix products  446 us (19%)
  local copies, waits for them, and re-layouts  87.5 us (4%)
  blocking collectives  86.6 us (4%)
  starting transfers between devices  79.3 us (3%)
  other arithmetic  52.2 us (2%)
    all_gather x1, waiting for transfers between devices, body(): lax.all_gather(w_up, 'seq', axis=0, tiled=True)  142 us
    reduce_scatter x1, waiting for transfers between devices, body(): lax.psum_scatter(grad_totals[10].astype(jnp.bfloat16), 'seq', scatter_dim...  141 us
    reduce_scatter x1, waiting for transfers between devices, body(): lax.psum_scatter(grad_totals[9].astype(jnp.bfloat16), 'seq', scatter_dime...  141 us
    all_gather x1, waiting for transfers between devices, body(): lax.all_gather(w_gate, 'seq', axis=0, tiled=True)  140 us
    all_gather x1, waiting for transfers between devices, body(): lax.all_gather(w_down, 'seq', axis=0, tiled=True)  136 us
    reduce_scatter x1, waiting for transfers between devices, body(): lax.psum_scatter(grad_totals[11].astype(jnp.bfloat16), 'seq', scatter_dim...  106 us
    reduce_scatter x1, waiting for transfers between devices, body(): lax.psum_scatter(grad_totals[1].astype(jnp.bfloat16), 'head', scatter_dim...  56.2 us
    all_to_all x2, waiting for transfers between devices, body(): lax.all_to_all(grad_copy.astype(jnp.bfloat16).reshape(head_count, slot_co...  54.9 us
  transfers between devices with their start and end apart: 51, of which 38 were waited for; matrix products, arithmetic and copies ran while one was open for 23% of the time, Pallas kernels for 0%

commit v1 on v0

v1 whole, which is shorter than its diff:
```python
import jax
import jax.numpy as jnp
from jax import lax
from jax.experimental import pallas as pl
from jax.experimental.pallas import tpu as pltpu
from jax.sharding import PartitionSpec as P

H = 16
HD = 128
TOPK = 8

eps = 1e-06
rope_base = 10000.0
bf16 = jnp.bfloat16
f32 = jnp.float32


def rms_scale(values):
    return lax.rsqrt(jnp.mean(values * values, axis=-1, keepdims=True) + eps)


def norm_back(grad_normed, normed, scale_rows):
    return scale_rows * (
        grad_normed - normed * jnp.mean(grad_normed * normed, axis=-1, keepdims=True)
    )


def swap(value, axis, bit):
    count = lax.axis_size(axis)
    return lax.ppermute(value, axis, [(i, i ^ (1 << bit)) for i in range(count)])


def bits_of(count):
    return count.bit_length() - 1


def spread(value, axis, order):
    bits = bits_of(lax.axis_size(axis))
    value = value.reshape((1,) * bits + value.shape)
    for bit in order:
        value = jnp.concatenate([value, swap(value, axis, bit)], axis=bits - 1 - bit)
    lead = 1
    for d in value.shape[:bits]:
        lead *= d
    return value.reshape((lead,) + value.shape[bits:])


def collect(value, axis, order, low=0):
    bits = bits_of(lax.axis_size(axis))
    rest = value.shape[1:]
    value = value.reshape((2,) * (bits - low) + (1,) * low + rest)
    for bit in order:
        at = bits - 1 - bit
        kept = lax.slice_in_dim(value, 0, 1, axis=at)
        sent = lax.slice_in_dim(value, 1, 2, axis=at)
        got = swap(sent, axis, bit)
        value = (kept.astype(f32) + got.astype(f32)).astype(value.dtype)
    return value.reshape(rest)


def total_over(value, axis, at):
    bits = bits_of(lax.axis_size(axis))
    shape = value.shape
    value = value.reshape(shape[:at] + (2,) * bits + shape[at + 1 :])
    for bit in range(bits):
        value = value + jnp.flip(swap(value, axis, bit), at + bits - 1 - bit)
    return value.reshape(shape)


def spread_halves(rows, axis, order):
    half = rows.shape[-2] // 2
    first = spread(rows[..., :half, :], axis, order)
    second = spread(rows[..., half:, :], axis, order[::-1])
    return jnp.concatenate([first, second], axis=-2)


def collect_halves(rows, axis, order, low):
    half = rows.shape[-2] // 2
    first = collect(rows[..., :half, :], axis, order[::-1], low)
    second = collect(rows[..., half:, :], axis, order, low)
    return jnp.concatenate([first, second], axis=-2)


def rotate(values, cosine, sine):
    half_width = HD // 2
    first_half = values[..., :half_width]
    second = values[..., half_width:]
    return jnp.concatenate(
        [first_half * cosine - second * sine, second * cosine + first_half * sine], axis=-1
    )


def segment_of(positions, lengths):
    count = lengths.shape[0]
    earlier = jnp.arange(count)[:, None] < jnp.arange(count)[None, :]
    starts = jnp.sum(jnp.where(earlier, lengths[:, None], 0), axis=0)
    return jnp.sum((positions[:, None] >= starts[None, :]).astype(jnp.int32), axis=1) - 1


score_scale = HD ** (-0.5)
by_rows = (((1,), (1,)), ((), ()))
by_first = (((0,), (0,)), ((), ()))


def attend_kernel(q_ref, k_ref, v_ref, sq_ref, sk_ref, o_ref, total_ref):
    scores = score_scale * lax.dot_general(
        q_ref[...], k_ref[...], by_rows, preferred_element_type=f32
    )
    scores = jnp.where(sq_ref[...] == sk_ref[...], scores, -1e30)
    most = jnp.max(scores, axis=1, keepdims=True)
    weights = jnp.exp(scores - most)
    total = jnp.sum(weights, axis=1, keepdims=True)
    mixed = jnp.dot(weights.astype(bf16), v_ref[...], preferred_element_type=f32)
    o_ref[...] = (mixed / total).astype(bf16)
    total_ref[...] = most + jnp.log(total)


def attend_back_kernel(
    q_ref, k_ref, v_ref, sq_ref, sk_ref, total_ref, g_ref, dq_ref, dk_ref, dv_ref, k_sum, v_sum
):
    step = pl.program_id(0)

    @pl.when(step == 0)
    def _():
        k_sum[...] = jnp.zeros_like(k_sum)
        v_sum[...] = jnp.zeros_like(v_sum)

    scores = score_scale * lax.dot_general(
        q_ref[...], k_ref[...], by_rows, preferred_element_type=f32
    )
    scores = jnp.where(sq_ref[...] == sk_ref[...], scores, -1e30)
    probs = jnp.exp(scores - total_ref[...])
    grad_probs = lax.dot_general(g_ref[...], v_ref[...], by_rows, preferred_element_type=f32)
    inner = jnp.sum(probs * grad_probs, axis=1, keepdims=True)
    grad_scores = (probs * (grad_probs - inner)).astype(bf16)
    dq_ref[...] = (
        score_scale * jnp.dot(grad_scores, k_ref[...], preferred_element_type=f32)
    ).astype(bf16)
    k_sum[...] += score_scale * lax.dot_general(
        grad_scores, q_ref[...], by_first, preferred_element_type=f32
    )
    v_sum[...] += lax.dot_general(
        probs.astype(bf16), g_ref[...], by_first, preferred_element_type=f32
    )

    @pl.when(step == pl.num_programs(0) - 1)
    def _():
        dk_ref[...] = k_sum[...].astype(bf16)
        dv_ref[...] = v_sum[...].astype(bf16)


def attend(queries, keys, values, seg_query, seg_key):
    rows, count = queries.shape[0], keys.shape[0]
    block = max(32, min(256, (1 << 19) // count, rows))
    by_block = lambda i: (i, 0)
    whole = lambda i: (0, 0)
    return pl.pallas_call(
        attend_kernel,
        grid=(rows // block,),
        in_specs=[
            pl.BlockSpec((block, HD), by_block),
            pl.BlockSpec((count, HD), whole),
            pl.BlockSpec((count, HD), whole),
            pl.BlockSpec((block, 1), by_block),
            pl.BlockSpec((1, count), whole),
        ],
        out_specs=[pl.BlockSpec((block, HD), by_block), pl.BlockSpec((block, 1), by_block)],
        out_shape=[
            jax.ShapeDtypeStruct((rows, HD), bf16),
            jax.ShapeDtypeStruct((rows, 1), f32),
        ],
        compiler_params=pltpu.CompilerParams(vmem_limit_bytes=40 << 20),
        name="attend",
    )(queries, keys, values, seg_query[:, None], seg_key[None, :])


def attend_back(queries, keys, values, seg_query, seg_key, totals, grad_mixed):
    rows, count = queries.shape[0], keys.shape[0]
    block = max(32, min(256, (1 << 19) // count, rows))
    by_block = lambda i: (i, 0)
    whole = lambda i: (0, 0)
    return pl.pallas_call(
        attend_back_kernel,
        grid=(rows // block,),
        in_specs=[
            pl.BlockSpec((block, HD), by_block),
            pl.BlockSpec((count, HD), whole),
            pl.BlockSpec((count, HD), whole),
            pl.BlockSpec((block, 1), by_block),
            pl.BlockSpec((1, count), whole),
            pl.BlockSpec((block, 1), by_block),
            pl.BlockSpec((block, HD), by_block),
        ],
        out_specs=[
            pl.BlockSpec((block, HD), by_block),
            pl.BlockSpec((count, HD), whole),
            pl.BlockSpec((count, HD), whole),
        ],
        out_shape=[
            jax.ShapeDtypeStruct((rows, HD), bf16),
            jax.ShapeDtypeStruct((count, HD), bf16),
            jax.ShapeDtypeStruct((count, HD), bf16),
        ],
        scratch_shapes=[pltpu.VMEM((count, HD), f32), pltpu.VMEM((count, HD), f32)],
        compiler_params=pltpu.CompilerParams(vmem_limit_bytes=48 << 20),
        name="attend_back",
    )(queries, keys, values, seg_query[:, None], seg_key[None, :], totals, grad_mixed)


def body(
    hidden_in,
    doc_lengths,
    expert_ids,
    out_grad,
    norm1_gain,
    w_query,
    w_key,
    w_value,
    query_gain,
    key_gain,
    w_out,
    norm2_gain,
    w_router,
    w_gate,
    w_up,
    w_down,
):
    heads_of = lax.axis_size("head")
    seqs = lax.axis_size("seq")
    head_index = lax.axis_index("head")
    seq_index = lax.axis_index("seq")
    micros, local, width = hidden_in.shape
    heads_here = H // heads_of
    cols = heads_here * HD
    experts_here = w_gate.shape[1]
    expert_count = experts_here * heads_of
    hidden_units = w_gate.shape[2]
    part_units = hidden_units // seqs
    tokens = micros * local
    stride = seqs * local
    slice_rows = heads_of * local
    head_bits = list(range(bits_of(heads_of)))
    chip_bits = head_bits[1:]
    seq_bits = list(range(bits_of(seqs)))
    row_iota = jnp.arange(local, dtype=jnp.int32)
    slots = jnp.arange(heads_of, dtype=jnp.int32)

    gain_one = norm1_gain.astype(f32)
    gain_two = norm2_gain.astype(f32)
    gain_query = lax.dynamic_slice(query_gain, (head_index * cols,), (cols,)).astype(f32)
    gain_key = lax.dynamic_slice(key_gain, (head_index * cols,), (cols,)).astype(f32)

    stacked = jnp.stack([w_query, w_key, w_value], axis=1)
    stacked = stacked.reshape(-1, 3, heads_of, cols).transpose(2, 0, 1, 3)
    weight_rows = stacked.shape[1]
    stacked = lax.all_to_all(
        stacked.reshape(heads_of, weight_rows, 3 * cols),
        "head",
        split_axis=0,
        concat_axis=0,
        tiled=True,
    )
    w_qkv = lax.all_gather(stacked, "seq", axis=1, tiled=True).reshape(width, 3 * cols)
    w_out_here = lax.all_gather(w_out, "seq", axis=0, tiled=True)

    def to_units(weight):
        rows = weight.shape[0]
        parts = weight.reshape(rows, experts_here, seqs, part_units).transpose(2, 0, 1, 3)
        parts = lax.all_to_all(
            parts.reshape(seqs, rows, experts_here * part_units),
            "seq",
            split_axis=0,
            concat_axis=0,
            tiled=True,
        )
        return parts.reshape(seqs * rows, experts_here * part_units)

    def both_cores(mine):
        return jnp.concatenate([mine, swap(mine, "head", 0)], axis=1)

    w_down_here = both_cores(to_units(w_down))
    w_gate_here = both_cores(to_units(w_gate))
    w_up_here = both_cores(to_units(w_up))
    w_gate_up = jnp.concatenate([w_gate_here, w_up_here], axis=1)
    unit_count = w_gate_here.shape[1]

    def gather_tokens(rows):
        rows = spread(rows, "seq", seq_bits[::-1])
        rows = spread_halves(rows, "head", chip_bits)
        return rows.reshape(-1, rows.shape[-1])

    def return_tokens(rows, length):
        rows = rows.reshape(heads_of // 2, seqs, length, rows.shape[-1])
        rows = collect_halves(rows, "head", chip_bits, 1)
        return collect(rows, "seq", seq_bits)

    grads_here = [gather_tokens(out_grad[m]) for m in range(micros)]

    def over_heads(sums):
        sums = total_over(sums.reshape(2, micros, heads_of, local), "head", 2)
        return sums.reshape(2, micros * slice_rows) / (heads_of * cols)

    hidden = hidden_in.reshape(tokens, width).astype(f32)
    scale_one = rms_scale(hidden)
    normed_one = hidden * scale_one
    act_one = (normed_one * gain_one).astype(bf16).reshape(micros, local, width)
    ag_order = chip_bits + [0]
    other_order = chip_bits[::-1] + [0]
    act_parts = [
        spread(act_one[m], "head", ag_order if m % 2 == 0 else other_order).reshape(
            slice_rows, width
        )
        for m in range(micros)
    ]
    act_slice = jnp.concatenate(act_parts, axis=0)
    qkv = jnp.dot(act_slice, w_qkv, preferred_element_type=f32)
    query_pre, key_pre, value_pre = qkv[:, :cols], qkv[:, cols : 2 * cols], qkv[:, 2 * cols :]
    squares = jnp.stack([jnp.sum(query_pre * query_pre, axis=1), jnp.sum(key_pre * key_pre, axis=1)])
    squares = over_heads(squares)
    query_scale = lax.rsqrt(squares[0] + eps)[:, None]
    key_scale = lax.rsqrt(squares[1] + eps)[:, None]
    query_normed = query_pre * query_scale
    key_normed = key_pre * key_scale

    slot_pos = ((head_index ^ slots) * stride + seq_index * local)[:, None] + row_iota[None, :]
    slot_pos = slot_pos.reshape(slice_rows)
    frequency = rope_base ** (-jnp.arange(HD // 2, dtype=f32) * 2.0 / HD)
    angles = slot_pos.astype(f32)[:, None] * frequency[None, :]
    cosine, sine = jnp.cos(angles), jnp.sin(angles)

    def turn(values, direction):
        shaped = values.reshape(micros, slice_rows, heads_here, HD)
        turned = rotate(shaped, cosine[None, :, None, :], direction * sine[None, :, None, :])
        return turned.reshape(values.shape)

    query_rot = turn(query_normed * gain_query, 1.0).astype(bf16)
    key_rot = turn(key_normed * gain_key, 1.0).astype(bf16)
    value_low = value_pre.astype(bf16)

    paired = heads_here * micros == seqs
    combos = heads_here * micros

    def to_pairs(values):
        kinds = values.shape[1] // cols
        values = values.reshape(micros, slice_rows, kinds, heads_here, HD)
        values = values.transpose(3, 0, 1, 2, 4).reshape(combos, slice_rows, kinds * HD)
        values = lax.all_to_all(values, "seq", split_axis=0, concat_axis=0, tiled=True)
        return values.reshape(seqs * slice_rows, kinds * HD)

    def from_pairs(values):
        kinds = values.shape[1] // HD
        values = lax.all_to_all(
            values.reshape(seqs, slice_rows, kinds * HD),
            "seq",
            split_axis=0,
            concat_axis=0,
            tiled=True,
        )
        values = values.reshape(heads_here, micros, slice_rows, kinds, HD)
        return values.transpose(1, 2, 3, 0, 4).reshape(micros * slice_rows, kinds * cols)

    all_pos = (
        ((head_index ^ slots) * stride)[None, :, None]
        + (jnp.arange(seqs, dtype=jnp.int32) * local)[:, None, None]
        + row_iota[None, None, :]
    ).reshape(seqs * slice_rows)
    if paired:
        triple = to_pairs(jnp.concatenate([query_rot, key_rot, value_low], axis=1))
        queries, keys, values = triple[:, :HD], triple[:, HD : 2 * HD], triple[:, 2 * HD :]
        segments = segment_of(all_pos, lax.dynamic_index_in_dim(doc_lengths, seq_index % micros, 0, False))
        mixed, totals = attend(queries, keys, values, segments, segments)
        mixed_slice = from_pairs(mixed)
    else:
        keys_all = lax.all_gather(key_rot.reshape(micros, slice_rows, cols), "seq", axis=1, tiled=True)
        values_all = lax.all_gather(value_low.reshape(micros, slice_rows, cols), "seq", axis=1, tiled=True)
        jobs = []
        pieces = []
        for m in range(micros):
            seg_key = segment_of(all_pos, doc_lengths[m])
            seg_query = segment_of(slot_pos, doc_lengths[m])
            row = []
            for a in range(heads_here):
                part = slice(a * HD, (a + 1) * HD)
                job = (
                    query_rot[m * slice_rows : (m + 1) * slice_rows, part],
                    keys_all[m][:, part],
                    values_all[m][:, part],
                    seg_query,
                    seg_key,
                )
                mixed, totals = attend(*job)
                jobs.append(job + (totals,))
                row.append(mixed)
            pieces.append(jnp.concatenate(row, axis=1))
        mixed_slice = jnp.concatenate(pieces, axis=0)

    def to_owner(partial):
        done = []
        for m in range(micros):
            part = partial[m * slice_rows : (m + 1) * slice_rows].reshape(heads_of, local, width)
            order = ag_order if m % 2 == 0 else other_order
            done.append(collect(part, "head", order[::-1]))
        return jnp.concatenate(done, axis=0).astype(f32)

    branch = to_owner(jnp.dot(mixed_slice, w_out_here, preferred_element_type=f32).astype(bf16))
    residual = hidden + branch
    scale_two = rms_scale(residual)
    normed_two = residual * scale_two
    act_two = (normed_two * gain_two).astype(bf16)
    logits = jnp.dot(act_two, w_router, preferred_element_type=f32)
    router_probs = jax.nn.softmax(logits, axis=-1)
    ids = expert_ids.reshape(tokens, TOPK)
    chosen = jnp.sum(
        (ids[:, :, None] == jnp.arange(expert_count, dtype=jnp.int32)[None, None, :]).astype(f32), axis=1
    )
    shares = (chosen * router_probs).reshape(micros, local, expert_count)

    def my_columns(table, index):
        return lax.dynamic_slice(table, (0, index * experts_here), (table.shape[0], experts_here))

    def widen(values):
        return jnp.repeat(values, part_units, axis=1)

    shares_all = spread(spread(jnp.swapaxes(shares, 0, 1), "seq", seq_bits[::-1]), "head", chip_bits)
    grad_acts, grad_routers, out_rows, states = [], [], [], []
    acts_here = []
    for m in range(micros):
        acts = gather_tokens(act_two.reshape(micros, local, width)[m])
        grads = grads_here[m]
        table = shares_all[:, :, :, m].reshape(-1, expert_count)
        gates = jnp.concatenate(
            [my_columns(table, head_index), my_columns(table, head_index ^ 1)], axis=1
        )
        gate_wide = widen(gates)
        gate_up = jnp.dot(acts, w_gate_up, preferred_element_type=f32)
        gate_pre, upward = gate_up[:, :unit_count], gate_up[:, unit_count:]
        grad_plain = jnp.dot(grads, w_down_here, preferred_element_type=f32)
        sigmoid_gate = jax.nn.sigmoid(gate_pre)
        inner = gate_pre * sigmoid_gate * upward
        inner_low = (inner * gate_wide).astype(bf16)
        grad_gate = jnp.sum((inner * grad_plain).reshape(-1, 2 * experts_here, part_units), axis=2)
        grad_inner = grad_plain * gate_wide
        grad_pre = (
            grad_inner * upward * sigmoid_gate * (1.0 + gate_pre * (1.0 - sigmoid_gate))
        ).astype(bf16)
        grad_up = (grad_inner * gate_pre * sigmoid_gate).astype(bf16)
        grad_both = jnp.concatenate([grad_pre, grad_up], axis=1)
        grad_part = lax.dot_general(grad_both, w_gate_up, by_rows, preferred_element_type=f32)
        grad_acts.append(return_tokens(grad_part.astype(bf16), local))
        lanes = jnp.arange(expert_count, dtype=jnp.int32)[None, :]
        placed = jnp.zeros((grad_gate.shape[0], expert_count), f32)
        for a in range(2 * experts_here):
            owner = (head_index ^ (a // experts_here)) * experts_here + a % experts_here
            placed = placed + jnp.where(lanes == owner, grad_gate[:, a : a + 1], 0.0)
        grad_routers.append(placed)
        out_part = lax.dot_general(inner_low, w_down_here, by_rows, preferred_element_type=f32)
        out_rows.append(return_tokens(out_part.astype(bf16), local))
        states.append((acts, grads, grad_both, inner_low))

    routers = jnp.stack(
        [r.reshape(heads_of // 2, seqs, local, expert_count) for r in grad_routers], axis=2
    )
    routers = collect(collect(routers, "head", chip_bits[::-1], 1), "seq", seq_bits)
    grad_router = routers.reshape(tokens, expert_count) * chosen
    expert_sum = jnp.concatenate(out_rows, axis=0).astype(f32)
    hidden_out = (residual + expert_sum).astype(bf16).reshape(micros, local, width)

    def weight_sum(pairs):
        total = None
        for left, right in pairs:
            part = lax.dot_general(left, right, by_first, preferred_element_type=f32)
            total = part if total is None else total + part
        return total

    def from_units(total):
        half = total.shape[1] // 2
        total = total[:, :half] + swap(total[:, half:].astype(bf16), "head", 0).astype(f32)
        parts = total.astype(bf16).reshape(seqs, width // seqs, experts_here * part_units)
        parts = lax.all_to_all(parts, "seq", split_axis=0, concat_axis=0, tiled=True)
        parts = parts.reshape(seqs, width // seqs, experts_here, part_units).transpose(1, 2, 0, 3)
        return parts.reshape(width // seqs, experts_here, hidden_units).astype(f32)

    grad_w_down = from_units(weight_sum([(s[1], s[3]) for s in states]))
    grad_gate_up = weight_sum([(s[0], s[2]) for s in states])
    grad_w_gate = from_units(grad_gate_up[:, :unit_count])
    grad_w_up = from_units(grad_gate_up[:, unit_count:])

    grad_logits = (
        router_probs * (grad_router - jnp.sum(router_probs * grad_router, axis=-1, keepdims=True))
    ).astype(bf16)
    grad_w_router = lax.dot_general(act_two, grad_logits, by_first, preferred_element_type=f32)
    grad_act_two = jnp.concatenate(grad_acts, axis=0).astype(f32) + lax.dot_general(
        grad_logits, w_router, by_rows, preferred_element_type=f32
    )
    grad_gain_two = jnp.sum(grad_act_two * normed_two, axis=0)
    grad_residual = out_grad.reshape(tokens, width).astype(f32) + norm_back(
        grad_act_two * gain_two, normed_two, scale_two
    )
    grad_branch = grad_residual.astype(bf16).reshape(micros, local, width)

    branch_slice = jnp.concatenate(
        [
            spread(grad_branch[m], "head", ag_order if m % 2 == 0 else other_order).reshape(
                slice_rows, width
            )
            for m in range(micros)
        ],
        axis=0,
    )
    grad_mixed = lax.dot_general(
        branch_slice, w_out_here, by_rows, preferred_element_type=f32
    ).astype(bf16)
    grad_w_out = lax.dot_general(mixed_slice, branch_slice, by_first, preferred_element_type=f32)
    grad_w_out = lax.psum_scatter(
        grad_w_out.astype(bf16), "seq", scatter_dimension=0, tiled=True
    ).astype(f32)
    if paired:
        grads3 = attend_back(queries, keys, values, segments, segments, totals, to_pairs(grad_mixed))
        back = from_pairs(jnp.concatenate(grads3, axis=1))
        back_query, back_key, back_value = back[:, :cols], back[:, cols : 2 * cols], back[:, 2 * cols :]
    else:
        back_query, back_key, back_value = [], [], []
        for m in range(micros):
            trio = [[], [], []]
            for a in range(heads_here):
                part = grad_mixed[m * slice_rows : (m + 1) * slice_rows, a * HD : (a + 1) * HD]
                for kept, grad in zip(trio, attend_back(*jobs[m * heads_here + a], part)):
                    kept.append(grad)
            dq, dk, dv = [jnp.concatenate(kept, axis=1) for kept in trio]
            back_query.append(dq)
            back_key.append(lax.psum_scatter(dk, "seq", scatter_dimension=0, tiled=True))
            back_value.append(lax.psum_scatter(dv, "seq", scatter_dimension=0, tiled=True))
        back_query, back_key, back_value = [
            jnp.concatenate(parts, axis=0) for parts in (back_query, back_key, back_value)
        ]

    grad_query_rot = turn(back_query.astype(f32), -1.0)
    grad_key_rot = turn(back_key.astype(f32), -1.0)
    grad_gain_query = jnp.sum(grad_query_rot * query_normed, axis=0)
    grad_gain_key = jnp.sum(grad_key_rot * key_normed, axis=0)
    pull_query = grad_query_rot * gain_query
    pull_key = grad_key_rot * gain_key
    means = jnp.stack(
        [jnp.sum(pull_query * query_normed, axis=1), jnp.sum(pull_key * key_normed, axis=1)]
    )
    means = over_heads(means)
    grad_query_pre = (query_scale * (pull_query - query_normed * means[0][:, None])).astype(bf16)
    grad_key_pre = (key_scale * (pull_key - key_normed * means[1][:, None])).astype(bf16)
    grad_qkv = jnp.concatenate([grad_query_pre, grad_key_pre, back_value], axis=1)
    grad_act = to_owner(
        lax.dot_general(grad_qkv, w_qkv, by_rows, preferred_element_type=f32).astype(bf16)
    )
    grad_w_qkv = lax.dot_general(act_slice, grad_qkv, by_first, preferred_element_type=f32)
    grad_w_qkv = lax.psum_scatter(
        grad_w_qkv.astype(bf16).reshape(heads_of, seqs, weight_rows, 3 * cols),
        "seq",
        scatter_dimension=1,
        tiled=True,
    ).reshape(heads_of, weight_rows, 3 * cols)
    grad_w_qkv = lax.all_to_all(grad_w_qkv, "head", split_axis=0, concat_axis=0, tiled=True)
    grad_w_qkv = grad_w_qkv.reshape(heads_of, weight_rows, 3, cols).transpose(2, 1, 0, 3)
    grad_w_qkv = grad_w_qkv.reshape(3, weight_rows, width).astype(f32)

    grad_gain_one = jnp.sum(grad_act * normed_one, axis=0)
    hidden_grad = grad_residual + norm_back(grad_act * gain_one, normed_one, scale_one)
    hidden_grad = hidden_grad.astype(bf16).reshape(micros, local, width)

    columns = jnp.concatenate([grad_w_router, grad_gain_two[:, None], grad_gain_one[:, None]], axis=1)
    columns = lax.psum_scatter(columns, "head", scatter_dimension=0, tiled=True)
    columns = jnp.concatenate([columns, grad_gain_query[:, None], grad_gain_key[:, None]], axis=1)
    columns = lax.psum_scatter(columns, "seq", scatter_dimension=0, tiled=True)
    return (
        hidden_out,
        hidden_grad,
        columns[:, expert_count + 1],
        grad_w_qkv[0],
        grad_w_qkv[1],
        grad_w_qkv[2],
        columns[:, expert_count + 2],
        columns[:, expert_count + 3],
        grad_w_out,
        columns[:, expert_count],
        columns[:, :expert_count],
        grad_w_gate,
        grad_w_up,
        grad_w_down,
    )


def solution(mesh):
    rows = P(("head", "seq"), None)
    blocks = P(None, ("head", "seq"), None)
    units = P("seq", "head", None)
    vector = P(("head", "seq"))
    in_specs = (
        blocks,
        P(),
        blocks,
        blocks,
        P(),
        rows,
        rows,
        rows,
        P(),
        P(),
        rows,
        P(),
        P(),
        units,
        units,
        units,
    )
    out_specs = (
        blocks,
        blocks,
        vector,
        rows,
        rows,
        rows,
        vector,
        vector,
        rows,
        vector,
        rows,
        units,
        units,
        units,
    )
    return jax.shard_map(body, mesh=mesh, in_specs=in_specs, out_specs=out_specs, check_vma=False)
```

time: 2300 us -> 1260 us (0.55)
  waiting for transfers between devices: 1520 us -> 529 us
  matrix products: 446 us -> 178 us
  local copies, waits for them, and re-layouts: 87.5 us -> 210 us
  other arithmetic: 52.2 us -> 132 us
  blocking collectives: 86.6 us -> 17.9 us
  starting transfers between devices: 79.3 us -> 143 us
  Pallas kernels: 0 us -> 26.3 us
    all_gather x15 -> x2, waiting for transfers between devices: 710 us -> 31.7 us  [the longest x1 31.7 us: body(): lax.all_gather(stacked, 'seq', axis=1, tiled=True).reshape(width, 3 * cols)]
    reduce_scatter x16 -> x3, waiting for transfers between devices: 598 us -> 0.02 us  [the longest x1 0.02 us: body(): lax.psum_scatter(grad_w_qkv.astype(bf16).reshape(heads_of, seqs, weight_r...]
    ppermute x0 -> x92, waiting for transfers between devices: none -> 331 us  [swap(): return lax.ppermute(value, axis, [(i, i ^ 1 << bit) for i in range(count)])]
    dot_general x70 -> x21, matrix products: 446 us -> 178 us  [the longest x4 56.9 us: weight_sum(): part = lax.dot_general(left, right, by_first, preferred_element_type=f32)]
    ppermute x0 -> x92, starting transfers between devices: none -> 93.1 us  [swap(): return lax.ppermute(value, axis, [(i, i ^ 1 << bit) for i in range(count)])]
    concatenate x8 -> x58, other arithmetic: 3.7 us -> 59.5 us  [the longest x40 45.3 us: spread(): jnp.concatenate([value, swap(value, axis, bit)], axis=bits - 1 - bit)]
    all_to_all x19 -> x11, waiting for transfers between devices: 208 us -> 154 us  [the longest x3 78.8 us: from_units(): lax.all_to_all(parts, 'seq', split_axis=0, concat_axis=0, tiled=True)]
    unnamed x2 -> x0, blocking collectives: 36.9 us -> none
  transfers between devices with their start and end apart: 51 -> 109, of which waited for: 38 -> 49; matrix products, arithmetic and copies ran while one was open for 23% -> 33% of each run, Pallas kernels for 0% -> 2%
where the time goes in v1:
time: 1260 us; the launch traced here: 1250 us
  waiting for transfers between devices  529 us (42%)
  local copies, waits for them, and re-layouts  210 us (17%)
  matrix products  178 us (14%)
  starting transfers between devices  143 us (11%)
  other arithmetic  132 us (10%)
  Pallas kernels  26.3 us (2%)
  blocking collectives  17.9 us (1%)
  between operations  17.1 us (1%)
    ppermute x92, waiting for transfers between devices, swap(): return lax.ppermute(value, axis, [(i, i ^ 1 << bit) for i in range(count)])  331 us
    ppermute x92, starting transfers between devices, swap(): return lax.ppermute(value, axis, [(i, i ^ 1 << bit) for i in range(count)])  93.1 us
    all_to_all x3, waiting for transfers between devices, from_units(): lax.all_to_all(parts, 'seq', split_axis=0, concat_axis=0, tiled=True)  78.8 us
    dot_general x4, matrix products, weight_sum(): part = lax.dot_general(left, right, by_first, preferred_element_type=f32)  56.9 us
    convert_element_type x9, local copies, waits for them, and re-layouts, from_units(): return parts.reshape(width // seqs, experts_here, hidden_units).astype(f32)  55.6 us
    unnamed x283, local copies, waits for them, and re-layouts  50.5 us
    concatenate x40, other arithmetic, spread(): jnp.concatenate([value, swap(value, axis, bit)], axis=bits - 1 - bit)  45.3 us
    all_to_all x2, waiting for transfers between devices, to_pairs(): lax.all_to_all(values, 'seq', split_axis=0, concat_axis=0, tiled=True)  38.3 us
  transfers between devices with their start and end apart: 109, of which 49 were waited for; matrix products, arithmetic and copies ran while one was open for 33% of the time, Pallas kernels for 2%

profile of v1, /device:TPU:0, one launch (start us, length us, event | category | flops | bytes accessed | tf_op | source)
XLA Modules:
  0.0 1252.8 jit_solution(14326020541767075803)
XLA Ops:
  14.3 17.9 %all_to_all.60 = bf16[8,64,768]{2,1,0:T(8,128)(2,1)} all-to-all(bf16[8,64,768]{2,1,0:T(8,128)(2,1)S(1)} %reshape.862), channel_id=1, replica_groups=mesh['head'=8,'seq'=4] {'head'}, dimensions={0} | all-to-all | bytes 1572864 | tf_op jit(solution)/shard_map/all_to_all | solution.py:256
  43.2 10.6 collective-permute-done.4
  63.4 31.7 %all-gather.3.cloned.1.call-done = bf16[8,256,768]{2,1,0:T(8,128)(2,1)} async-done(((bf16[8,64,768]{2,1,0:T(8,128)(2,1)}), bf16[8,256,768]{2,1,0:T(8,128)(2,1)}) %all-gather.3.cloned.1.call-update) | async-done | bytes 3145744 | tf_op jit(solution)/shard_map/all_gather | solution.py:263
  135.9 38.3 %all-to-all-done.1 = bf16[4,512,384]{1,2,0:T(8,128)(2,1)S(1)} async-done(((bf16[4,512,384]{1,2,0:T(8,128)(2,1)}), bf16[4,512,384]{1,2,0:T(8,128)(2,1)S(1)}, u32[]{:S(2)}, u32[]{:S(2)}) %all-to-all-start.1) | async-done | bytes 1572896 | tf_op jit(solution)/shard_map/all_to_all | solution.py:347
  177.3 10.4 attend.1
  208.9 24.6 %collective-permute-done.58 = bf16[1,1,64,2048]{3,2,1,0:T(8,128)(2,1)S(1)} collective-permute-done((bf16[1,1,64,2048]{3,2,1,0:T(8,128)(2,1)S(1)}, bf16[1,1,64,2048]{3,2,1,0:T(8,128)(2,1)S(1)}, u32[]{:S(2)}, u32[]{:S(2)}) %collective-permute-start.58) | collective-permute-done | bytes 262176 | tf_op jit(solution)/shard_map/ppermute | solution.py:30
  250.9 19.3 %collective-permute-done.59 = bf16[2,1,64,2048]{3,2,1,0:T(8,128)(2,1)} collective-permute-done((bf16[2,1,64,2048]{3,2,1,0:T(8,128)(2,1)}, bf16[2,1,64,2048]{3,2,1,0:T(8,128)(2,1)}, u32[]{:S(2)}, u32[]{:S(2)}) %collective-permute-start.59) | collective-permute-done | bytes 524320 | tf_op jit(solution)/shard_map/ppermute | solution.py:30
  353.1 17.4 %all-to-all-done.3 = bf16[4,512,512]{1,2,0:T(8,128)(2,1)} async-done(((bf16[4,512,512]{1,2,0:T(8,128)(2,1)}), bf16[4,512,512]{1,2,0:T(8,128)(2,1)}, u32[]{:S(2)}, u32[]{:S(2)}) %all-to-all-start.3) | async-done | bytes 2097184 | tf_op jit(solution)/shard_map/all_to_all | solution.py:269
  382.4 41.7 %collective-permute-done.23 = f32[1,1,64,2,16]{2,3,4,1,0:T(2,128)S(1)} collective-permute-done((f32[1,1,64,2,16]{2,3,4,1,0:T(2,128)S(1)}, f32[1,1,64,2,16]{2,3,4,1,0:T(2,128)S(1)}, u32[]{:S(2)}, u32[]{:S(2)}) %collective-permute-start.23) | collective-permute-done | bytes 8224 | tf_op jit(solution)/shard_map/ppermute | solution.py:30
  521.0 15.5 %fusion.75 = f32[1024,2048]{1,0:T(8,128)} fusion(bf16[1024,2048]{1,0:T(8,128)(2,1)S(1)} %bitcast.428, bf16[2048,512]{1,0:T(8,128)(2,1)} %collective-permute-done.22, bf16[2048,512]{1,0:T(8,128)(2,1)} %bitcast.455, bf16[2048,512]{1,0:T(8,128)(2,1)} %collective-permute-done.21, bf16[2048,512]{1,0:T(8,128)(2,1)} %bitcast.460), kind=kOutput, calls=%fused_computation.337 | convolution fusion | flops 8623489024 | bytes 20971520 | tf_op jit(solution)/shard_map/dot_general | solution.py:435
  536.6 13.0 %multiply_convert_fusion.1 = (bf16[1024,1024]{1,0:T(8,128)(2,1)}, bf16[1024,1024]{1,0:T(8,128)(2,1)}, f32[1024,1024]{1,0:T(8,128)}, bf16[1024,1024]{1,0:T(8,128)(2,1)}) fusion(f32[1024,2048]{1,0:T(8,128)} %fusion.75, f32[1024,1024]{1,0:T(8,128)} %bitcast.433, bf16[1024,2048]{1,0:T(8,128)(2,1)S(1)} %bitcast.425, ...), kind=kOutput, calls=%fused_computation.22 | convolution fusion | flops 4323278848 | bytes 31457280 | tf_op jit(solution)/shard_map/dot_general | solution.py:437
  549.6 12.6 %convolution_convert_fusion = bf16[1024,2048]{1,0:T(8,128)(2,1)S(1)} fusion(bf16[1024,1024]{1,0:T(8,128)(2,1)} %get-tuple-element.51, bf16[1024,1024]{1,0:T(8,128)(2,1)} %get-tuple-element.50, bf16[2048,512]{1,0:T(8,128)(2,1)} %collective-permute-done.22, bf16[2048,512]{1,0:T(8,128)(2,1)} %bitcast.456, bf16[2048,512]{1,0:T(8,128)(2,1)} %collective-permute-done.21, ...), kind=kOutput, calls=%fused_computation.32 | convolution fusion | flops 8633974784 | bytes 16777216 | tf_op jit(solution)/shard_map/dot_general | solution.py:448
  570.9 15.5 %fusion.76 = f32[1024,2048]{1,0:T(8,128)} fusion(bf16[1024,2048]{1,0:T(8,128)(2,1)} %bitcast.431, bf16[2048,512]{1,0:T(8,128)(2,1)} %collective-permute-done.22, bf16[2048,512]{1,0:T(8,128)(2,1)S(1)} %bitcast.457, bf16[2048,512]{1,0:T(8,128)(2,1)} %collective-permute-done.21, bf16[2048,512]{1,0:T(8,128)(2,1)} %bitcast.462), kind=kOutput, calls=%fused_computation.338 | convolution fusion | flops 8623489024 | bytes 20971520 | tf_op jit(solution)/shard_map/dot_general | solution.py:435
  586.5 12.4 multiply_convert_fusion.3
  627.1 15.3 %fusion.5 = f32[2048,2048]{1,0:T(8,128)} fusion(bf16[1024,2048]{1,0:T(8,128)(2,1)} %bitcast.432, bf16[1024,1024]{1,0:T(8,128)(2,1)} %get-tuple-element.49, bf16[1024,1024]{1,0:T(8,128)(2,1)} %get-tuple-element.48), kind=kOutput, calls=%fused_computation.41 | convolution fusion | flops 8598323200 | bytes 25165824 | tf_op jit(solution)/shard_map/dot_general | solution.py:471
  642.4 19.0 %fusion.86 = (bf16[2048,2048]{1,0:T(8,128)(2,1)}, f32[2048,2048]{1,0:T(8,128)}) fusion(f32[2048,2048]{1,0:T(8,128)} %fusion.5, bf16[1024,2048]{1,0:T(8,128)(2,1)} %bitcast.429, bf16[1024,1024]{1,0:T(8,128)(2,1)} %get-tuple-element.51, bf16[1024,1024]{1,0:T(8,128)(2,1)} %get-tuple-element.50), kind=kOutput, calls=%fused_computation.348 | convolution fusion | flops 8606711808 | bytes 50331648 | tf_op jit(solution)/shard_map/dot_general | solution.py:471
  661.4 12.5 convolution_convert_fusion.1
  673.9 12.3 fusion.87
  713.8 16.0 %collective-permute-done.54 = bf16[2,1,1,4,32,2048]{5,4,3,2,1,0:T(8,128)(2,1)} collective-permute-done((bf16[2,1,1,4,32,2048]{5,4,3,2,1,0:T(8,128)(2,1)}, bf16[2,1,1,4,32,2048]{5,4,3,2,1,0:T(8,128)(2,1)}, u32[]{:S(2)}, u32[]{:S(2)}) %collective-permute-start.54) | collective-permute-done | bytes 1048608 | tf_op jit(solution)/shard_map/ppermute | solution.py:30
  735.9 27.0 %collective-permute-done.67 = bf16[1,1,1,4,32,2048]{5,4,3,2,1,0:T(8,128)(2,1)S(1)} collective-permute-done((bf16[1,1,1,4,32,2048]{5,4,3,2,1,0:T(8,128)(2,1)S(1)}, bf16[1,1,1,4,32,2048]{5,4,3,2,1,0:T(8,128)(2,1)S(1)}, u32[]{:S(2)}, u32[]{:S(2)}) %collective-permute-start.67) | collective-permute-done | bytes 524320 | tf_op jit(solution)/shard_map/ppermute | solution.py:30
  781.8 9.1 collective-permute-done.56
  791.2 9.0 collective-permute-done.57
  842.2 8.5 collective-permute-done.30
  856.1 15.9 %attend_back.1 = (bf16[2048,128]{1,0:T(8,128)(2,1)S(1)}, bf16[2048,128]{1,0:T(8,128)(2,1)S(1)}, bf16[2048,128]{1,0:T(8,128)(2,1)S(1)}) custom-call(bf16[2048,128]{1,0:T(8,128)(2,1)S(1)} %copy-done.6, bf16[2048,128]{1,0:T(8,128)(2,1)S(1)} %copy-done.4, bf16[2048,128]{1,0:T(8,128)(2,1)S(1)} %copy-done.2, s32[2048,1]{1,0:T(8,128)S(1)} %copy.202.sq_ref, ...), custom_call_target="tpu_custom_call" | custom-call | tf_op jit(solution)/shard_map/attend_back/pallas_call | solution.py:182
  894.8 19.9 %all-to-all-done.7 = bf16[4,512,384]{1,2,0:T(8,128)(2,1)S(1)} async-done(((bf16[4,512,384]{1,2,0:T(8,128)(2,1)}), bf16[4,512,384]{1,2,0:T(8,128)(2,1)S(1)}, u32[]{:S(2)}, u32[]{:S(2)}) %all-to-all-start.7) | async-done | bytes 1572896 | tf_op jit(solution)/shard_map/all_to_all | solution.py:352
  929.4 8.2 fusion.1
  958.4 50.1 %collective-permute-done.45 = bf16[1,1,64,2048]{3,2,1,0:T(8,128)(2,1)} collective-permute-done((bf16[1,1,64,2048]{3,2,1,0:T(8,128)(2,1)}, bf16[1,1,64,2048]{3,2,1,0:T(8,128)(2,1)}, u32[]{:S(2)}, u32[]{:S(2)}) %collective-permute-start.45) | collective-permute-done | bytes 262176 | tf_op jit(solution)/shard_map/ppermute | solution.py:30
  1052.0 10.3 convolution_add_fusion.1
  1069.1 42.0 %all-to-all-done.10 = bf16[4,512,512]{2,1,0:T(8,128)(2,1)S(1)} async-done(((bf16[4,512,512]{2,1,0:T(8,128)(2,1)}), bf16[4,512,512]{2,1,0:T(8,128)(2,1)S(1)}, u32[]{:S(2)}, u32[]{:S(2)}) %all-to-all-start.10) | async-done | bytes 2097184 | tf_op jit(solution)/shard_map/all_to_all | solution.py:479
  1111.1 8.6 all-to-all-start.11
  1156.2 36.7 %all-to-all-done.11 = bf16[4,512,512]{2,1,0:T(8,128)(2,1)} async-done(((bf16[4,512,512]{2,1,0:T(8,128)(2,1)}), bf16[4,512,512]{2,1,0:T(8,128)(2,1)}, u32[]{:S(2)}, u32[]{:S(2)}) %all-to-all-start.11) | async-done | bytes 2097184 | tf_op jit(solution)/shard_map/all_to_all | solution.py:479
  1221.5 12.0 reduce-scatter.13.cloned.1.call-done
  (789 shorter events, 622.2 us)
Async XLA Ops:
  7.2 88.0 %all-gather.3.cloned.1.call-start = ((), (), s32[]{:S(2)}) async-start(), calls=%async_computation.16 | async-start | bytes 3932160 | tf_op jit(solution)/shard_map/all_gather | solution.py:263
  132.2 61.2 %collective-permute-start.46 = (bf16[1,1,64,2048]{3,2,1,0:T(8,128)(2,1)}, bf16[1,1,64,2048]{3,2,1,0:T(8,128)(2,1)}, u32[]{:S(2)}, u32[]{:S(2)}) collective-permute-start(bf16[1,1,64,2048]{3,2,1,0:T(8,128)(2,1)} %get-tuple-element.94), channel_id=1, source_target_pairs={{0,2},{1,3},{2,0},{3,1},{4,6},{5,7},{6,4},{7,5},{8,10},{9,11},{10,... | collective-permute-start | bytes 786440 | tf_op jit(solution)/shard_map/ppermute | solution.py:30
  189.5 53.0 %all-to-all-start.2 = ((bf16[4,512,128]{2,1,0:T(8,128)(2,1)}), bf16[4,512,128]{2,1,0:T(8,128)(2,1)S(1)}, u32[]{:S(2)}, u32[]{:S(2)}) async-start(bf16[4,512,128]{2,1,0:T(8,128)(2,1)} %bitcast.13), calls=%async_computation.2 | async-start | bytes 1048576 | tf_op jit(solution)/shard_map/all_to_all | solution.py:352
  193.4 110.3 %all-gather.5.cloned.1.call-start = ((), (), s32[]{:S(2)}) async-start(), calls=%async_computation.17 | async-start | bytes 1310720 | tf_op jit(solution)/shard_map/all_gather | solution.py:264
  242.5 74.3 %all-to-all-start.4 = ((bf16[4,512,512]{1,2,0:T(8,128)(2,1)}), bf16[4,512,512]{1,2,0:T(8,128)(2,1)}, u32[]{:S(2)}, u32[]{:S(2)}) async-start(bf16[4,512,512]{1,2,0:T(8,128)(2,1)} %bitcast.365), calls=%async_computation.4 | async-start | bytes 4194304 | tf_op jit(solution)/shard_map/all_to_all | solution.py:269
  310.7 70.1 %collective-permute-start.61 = (bf16[1,2,1,4,32,2048]{5,4,3,2,1,0:T(8,128)(2,1)}, bf16[1,2,1,4,32,2048]{5,4,3,2,1,0:T(8,128)(2,1)}, u32[]{:S(2)}, u32[]{:S(2)}) collective-permute-start(bf16[1,2,1,4,32,2048]{5,4,3,2,1,0:T(8,128)(2,1)} %pad_maximum_fusion.49), channel_id=1, source_target_pairs={{0,16},{4,20},{8,24},{12,28},{16,0},{20,4},{24,8},{28,12},{1,17},{... | collective-permute-start | bytes 3145736 | tf_op jit(solution)/shard_map/ppermute | solution.py:30
  316.8 53.7 %all-to-all-start.3 = ((bf16[4,512,512]{1,2,0:T(8,128)(2,1)}), bf16[4,512,512]{1,2,0:T(8,128)(2,1)}, u32[]{:S(2)}, u32[]{:S(2)}) async-start(bf16[4,512,512]{1,2,0:T(8,128)(2,1)} %bitcast.364), calls=%async_computation.3 | async-start | bytes 4194304 | tf_op jit(solution)/shard_map/all_to_all | solution.py:269
  370.5 71.1 %all-to-all-start.5 = ((bf16[4,512,512]{1,2,0:T(8,128)(2,1)}), bf16[4,512,512]{1,2,0:T(8,128)(2,1)}, u32[]{:S(2)}, u32[]{:S(2)}) async-start(bf16[4,512,512]{1,2,0:T(8,128)(2,1)} %bitcast.363), calls=%async_computation.5 | async-start | bytes 4194304 | tf_op jit(solution)/shard_map/all_to_all | solution.py:269
  436.9 84.0 %collective-permute-start.22 = (bf16[2048,512]{1,0:T(8,128)(2,1)}, bf16[2048,512]{1,0:T(8,128)(2,1)}, u32[]{:S(2)}, u32[]{:S(2)}) collective-permute-start(bf16[2048,512]{1,0:T(8,128)(2,1)} %bitcast.454), channel_id=1, source_target_pairs={{0,4},{4,0},{8,12},{12,8},{16,20},{20,16},{24,28},{28,24},{1,5},{5... | collective-permute-start | bytes 6291464 | tf_op jit(solution)/shard_map/ppermute | solution.py:30
  441.1 79.9 %collective-permute-start.21 = (bf16[2048,512]{1,0:T(8,128)(2,1)}, bf16[2048,512]{1,0:T(8,128)(2,1)}, u32[]{:S(2)}, u32[]{:S(2)}) collective-permute-start(bf16[2048,512]{1,0:T(8,128)(2,1)} %bitcast.459), channel_id=1, source_target_pairs={{0,4},{4,0},{8,12},{12,8},{16,20},{20,16},{24,28},{28,24},{1,5},{5... | collective-permute-start | bytes 6291464 | tf_op jit(solution)/shard_map/ppermute | solution.py:30
  518.1 48.6 %collective-permute-start.18 = (bf16[1,2,1,4,32,2048]{5,4,3,2,1,0:T(8,128)(2,1)}, bf16[1,2,1,4,32,2048]{5,4,3,2,1,0:T(8,128)(2,1)}, u32[]{:S(2)}, u32[]{:S(2)}) collective-permute-start(bf16[1,2,1,4,32,2048]{5,4,3,2,1,0:T(8,128)(2,1)} %pad_maximum_fusion.40), channel_id=1, source_target_pairs={{0,16},{4,20},{8,24},{12,28},{16,0},{20,4},{24,8},{28,12},{1,17},{... | collective-permute-start | bytes 3145736 | tf_op jit(solution)/shard_map/ppermute | solution.py:30
  621.3 65.0 %collective-permute-start.70 = (f32[1,2,1,4,2,64,16]{5,4,6,3,2,1,0:T(2,128)}, f32[1,2,1,4,2,64,16]{5,4,6,3,2,1,0:T(2,128)}, u32[]{:S(2)}, u32[]{:S(2)}) collective-permute-start(f32[1,2,1,4,2,64,16]{5,4,6,3,2,1,0:T(2,128)} %fusion.54), channel_id=1, source_target_pairs={{0,16},{4,20},{8,24},{12,28},{16,0},{20,4},{24,8},{28,12},{1,17},{... | collective-permute-start | bytes 196616 | tf_op jit(solution)/shard_map/ppermute | solution.py:30
  624.9 82.8 %collective-permute-start.66 = (bf16[2,1,1,4,32,2048]{5,4,3,2,1,0:T(8,128)(2,1)}, bf16[2,1,1,4,32,2048]{5,4,3,2,1,0:T(8,128)(2,1)}, u32[]{:S(2)}, u32[]{:S(2)}) collective-permute-start(bf16[2,1,1,4,32,2048]{5,4,3,2,1,0:T(8,128)(2,1)} %slice.764), channel_id=1, source_target_pairs={{0,8},{4,12},{8,0},{12,4},{16,24},{20,28},{24,16},{28,20},{1,9},{5... | collective-permute-start | bytes 3145736 | tf_op jit(solution)/shard_map/ppermute | solution.py:30
  626.3 84.4 %collective-permute-start.64 = (bf16[1,2,1,4,32,2048]{5,4,3,1,2,0:T(8,128)(2,1)}, bf16[1,2,1,4,32,2048]{5,4,3,1,2,0:T(8,128)(2,1)}, u32[]{:S(2)}, u32[]{:S(2)}) collective-permute-start(bf16[1,2,1,4,32,2048]{5,4,3,1,2,0:T(8,128)(2,1)} %slice_bitcast_fusion), channel_id=1, source_target_pairs={{0,16},{4,20},{8,24},{12,28},{16,0},{20,4},{24,8},{28,12},{1,17},{... | collective-permute-start | bytes 3145736 | tf_op jit(solution)/shard_map/ppermute | solution.py:30
  706.9 119.5 %collective-permute-start.42 = (bf16[2,1,1,4,32,2048]{5,4,3,1,0,2:T(8,128)(2,1)}, bf16[2,1,1,4,32,2048]{5,4,3,1,0,2:T(8,128)(2,1)}, u32[]{:S(2)}, u32[]{:S(2)}) collective-permute-start(bf16[2,1,1,4,32,2048]{5,4,3,1,0,2:T(8,128)(2,1)} %slice.734), channel_id=1, source_target_pairs={{0,8},{4,12},{8,0},{12,4},{16,24},{20,28},{24,16},{28,20},{1,9},{5... | collective-permute-start | bytes 3145736 | tf_op jit(solution)/shard_map/ppermute | solution.py:30
  707.7 130.5 %collective-permute-start.40 = (bf16[1,2,1,4,32,2048]{5,4,3,1,2,0:T(8,128)(2,1)}, bf16[1,2,1,4,32,2048]{5,4,3,1,2,0:T(8,128)(2,1)}, u32[]{:S(2)}, u32[]{:S(2)}) collective-permute-start(bf16[1,2,1,4,32,2048]{5,4,3,1,2,0:T(8,128)(2,1)} %slice_bitcast_fusion.4), channel_id=1, source_target_pairs={{0,16},{4,20},{8,24},{12,28},{16,0},{20,4},{24,8},{28,12},{1,17},{... | collective-permute-start | bytes 3145736 | tf_op jit(solution)/shard_map/ppermute | solution.py:30
  710.7 52.3 %collective-permute-start.67 = (bf16[1,1,1,4,32,2048]{5,4,3,2,1,0:T(8,128)(2,1)S(1)}, bf16[1,1,1,4,32,2048]{5,4,3,2,1,0:T(8,128)(2,1)S(1)}, u32[]{:S(2)}, u32[]{:S(2)}) collective-permute-start(bf16[1,1,1,4,32,2048]{5,4,3,2,1,0:T(8,128)(2,1)S(1)} %slice.766), channel_id=1, source_target_pairs={{0,16},{4,20},{8,24},{12,28},{16,0},{20,4},{24,8},{28,12},{1,17},{... | collective-permute-start | bytes 1572872 | tf_op jit(solution)/shard_map/ppermute | solution.py:30
  826.3 51.4 %collective-permute-start.28 = (bf16[1,2,1,4,32,2048]{5,4,3,1,2,0:T(8,128)(2,1)}, bf16[1,2,1,4,32,2048]{5,4,3,1,2,0:T(8,128)(2,1)}, u32[]{:S(2)}, u32[]{:S(2)}) collective-permute-start(bf16[1,2,1,4,32,2048]{5,4,3,1,2,0:T(8,128)(2,1)} %slice_bitcast_fusion.6), channel_id=1, source_target_pairs={{0,16},{4,20},{8,24},{12,28},{16,0},{20,4},{24,8},{28,12},{1,17},{... | collective-permute-start | bytes 3145736 | tf_op jit(solution)/shard_map/ppermute | solution.py:30
  830.1 99.3 %collective-permute-start.90 = (bf16[2048,512]{1,0:T(8,128)(2,1)}, bf16[2048,512]{1,0:T(8,128)(2,1)}, u32[]{:S(2)}, u32[]{:S(2)}) collective-permute-start(bf16[2048,512]{1,0:T(8,128)(2,1)} %get-tuple-element.56), channel_id=1, source_target_pairs={{0,4},{4,0},{8,12},{12,8},{16,20},{20,16},{24,28},{28,24},{1,5},{5... | collective-permute-start | bytes 6291464 | tf_op jit(solution)/shard_map/ppermute | solution.py:30
  830.3 99.1 %collective-permute-start.89 = (bf16[2048,512]{1,0:T(8,128)(2,1)}, bf16[2048,512]{1,0:T(8,128)(2,1)}, u32[]{:S(2)}, u32[]{:S(2)}) collective-permute-start(bf16[2048,512]{1,0:T(8,128)(2,1)} %get-tuple-element.57), channel_id=1, source_target_pairs={{0,4},{4,0},{8,12},{12,8},{16,20},{20,16},{24,28},{28,24},{1,5},{5... | collective-permute-start | bytes 6291464 | tf_op jit(solution)/shard_map/ppermute | solution.py:30
  885.8 57.4 %collective-permute-start.44 = (bf16[2,1,64,2048]{3,2,1,0:T(8,128)(2,1)}, bf16[2,1,64,2048]{3,2,1,0:T(8,128)(2,1)}, u32[]{:S(2)}, u32[]{:S(2)}) collective-permute-start(bf16[2,1,64,2048]{3,2,1,0:T(8,128)(2,1)} %pad_maximum_fusion.59), channel_id=1, source_target_pairs={{0,1},{1,0},{2,3},{3,2},{4,5},{5,4},{6,7},{7,6},{8,9},{9,8},{10,11... | collective-permute-start | bytes 1572872 | tf_op jit(solution)/shard_map/ppermute | solution.py:30
  937.6 110.8 %all-to-all-start.9 = ((bf16[4,512,512]{2,1,0:T(8,128)(2,1)}), bf16[4,512,512]{2,1,0:T(8,128)(2,1)}, u32[]{:S(2)}, u32[]{:S(2)}) async-start(bf16[4,512,512]{2,1,0:T(8,128)(2,1)} %bitcast.387), calls=%async_computation.12 | async-start | bytes 4194304 | tf_op jit(solution)/shard_map/all_to_all | solution.py:479
  942.0 270.1 %reduce-scatter.11.cloned.1.call-start = ((), (), s32[]{:S(2)}) async-start(), calls=%async_computation.20 | async-start | bytes 1310720 | tf_op jit(solution)/shard_map/reduce_scatter | solution.py:514
  946.1 62.4 %collective-permute-start.45 = (bf16[1,1,64,2048]{3,2,1,0:T(8,128)(2,1)}, bf16[1,1,64,2048]{3,2,1,0:T(8,128)(2,1)}, u32[]{:S(2)}, u32[]{:S(2)}) collective-permute-start(bf16[1,1,64,2048]{3,2,1,0:T(8,128)(2,1)} %slice.740), channel_id=1, source_target_pairs={{0,2},{1,3},{2,0},{3,1},{4,6},{5,7},{6,4},{7,5},{8,10},{9,11},{10,... | collective-permute-start | bytes 786440 | tf_op jit(solution)/shard_map/ppermute | solution.py:30
  956.4 57.4 %collective-permute-start.86 = (bf16[2,2,1,64,2048]{4,3,2,1,0:T(8,128)(2,1)S(1)}, bf16[2,2,1,64,2048]{4,3,2,1,0:T(8,128)(2,1)S(1)}, u32[]{:S(2)}, u32[]{:S(2)}) collective-permute-start(bf16[2,2,1,64,2048]{4,3,2,1,0:T(8,128)(2,1)S(1)} %slice.807), channel_id=1, source_target_pairs={{0,4},{4,0},{8,12},{12,8},{16,20},{20,16},{24,28},{28,24},{1,5},{5... | collective-permute-start | bytes 3145736 | tf_op jit(solution)/shard_map/ppermute | solution.py:30
  957.7 55.3 %collective-permute-start.33 = (bf16[1,1,64,2048]{3,2,1,0:T(8,128)(2,1)S(1)}, bf16[1,1,64,2048]{3,2,1,0:T(8,128)(2,1)S(1)}, u32[]{:S(2)}, u32[]{:S(2)}) collective-permute-start(bf16[1,1,64,2048]{3,2,1,0:T(8,128)(2,1)S(1)} %slice.721), channel_id=1, source_target_pairs={{0,2},{1,3},{2,0},{3,1},{4,6},{5,7},{6,4},{7,5},{8,10},{9,11},{10,... | collective-permute-start | bytes 786440 | tf_op jit(solution)/shard_map/ppermute | solution.py:30
  957.9 57.8 %collective-permute-start.83 = (bf16[2,2,1,64,2048]{4,3,2,1,0:T(8,128)(2,1)S(1)}, bf16[2,2,1,64,2048]{4,3,2,1,0:T(8,128)(2,1)S(1)}, u32[]{:S(2)}, u32[]{:S(2)}) collective-permute-start(bf16[2,2,1,64,2048]{4,3,2,1,0:T(8,128)(2,1)S(1)} %slice.800), channel_id=1, source_target_pairs={{0,4},{4,0},{8,12},{12,8},{16,20},{20,16},{24,28},{28,24},{1,5},{5... | collective-permute-start | bytes 3145736 | tf_op jit(solution)/shard_map/ppermute | solution.py:30
  1020.2 193.9 %reduce-scatter.7.cloned.1.call-start = ((), (), s32[]{:S(2)}) async-start(), calls=%async_computation.18 | async-start | bytes 221184 | tf_op jit(solution)/shard_map/reduce_scatter | solution.py:569
  1040.4 175.3 %reduce-scatter.9.cloned.1.call-start = ((), (), s32[]{:S(2)}) async-start(), calls=%async_computation.19 | async-start | bytes 3932160 | tf_op jit(solution)/shard_map/reduce_scatter | solution.py:554
  1048.4 62.7 %all-to-all-start.10 = ((bf16[4,512,512]{2,1,0:T(8,128)(2,1)}), bf16[4,512,512]{2,1,0:T(8,128)(2,1)S(1)}, u32[]{:S(2)}, u32[]{:S(2)}) async-start(bf16[4,512,512]{2,1,0:T(8,128)(2,1)} %bitcast.386), calls=%async_computation.13 | async-start | bytes 4194304 | tf_op jit(solution)/shard_map/all_to_all | solution.py:479
  1111.1 81.8 %all-to-all-start.11 = ((bf16[4,512,512]{2,1,0:T(8,128)(2,1)}), bf16[4,512,512]{2,1,0:T(8,128)(2,1)}, u32[]{:S(2)}, u32[]{:S(2)}) async-start(bf16[4,512,512]{2,1,0:T(8,128)(2,1)} %bitcast.380), calls=%async_computation.14 | async-start | bytes 4194304 | tf_op jit(solution)/shard_map/all_to_all | solution.py:479
  1119.8 113.8 %reduce-scatter.13.cloned.1.call-start = ((), (), s32[]{:S(2)}) async-start(), calls=%async_computation.21 | async-start | bytes 163840
  (206 other events, 3310.8 us)
Sparse Core Ops, SparseCore 0:
  32.3 62.8 all-gather.2
  199.1 37.8 all-gather.4
  1020.3 25.6 reduce-scatter.10
  1049.8 32.1 reduce-scatter.6
  1084.2 89.3 reduce-scatter.8
  1215.8 17.7 reduce-scatter.12
